TPU v7x, 256 devices: a whole 4x4x8 slice. The times are simulated.
256 devices in a mesh: tm: 32 (over y, z_lo, core), space: 8 (over z_hi, x).
Axes of the slice: x: 4, y: 4, z: 8 (z_hi: 2, z_lo: 4; z = z_hi * 4 + z_lo), core: 2. Of those that a mesh axis runs over, the one named last changes fastest.
Arguments:
- queries: bfloat16 [32768, 4096], P(('tm', 'space')), may hold values from -14 to 14
- keys: bfloat16 [32768, 2048], P(('tm', 'space')), may hold values from -6 to 6
- values: bfloat16 [32768, 2048], P(('tm', 'space')), may hold values from -6 to 6
- output_gradient: bfloat16 [32768, 4096], P(('tm', 'space')), may hold values from -6 to 6
- tiles: int32 [256, 6], P('tm'), may hold values from 0 to 23, as said below
- kinds: int32 [256, 6], P('tm'), may hold values from 0 to 2, as said below
Outputs:
- grad_queries: bfloat16 [32768, 4096], P(('tm', 'space'))
- grad_keys: bfloat16 [32768, 2048], P(('tm', 'space'))
- grad_values: bfloat16 [32768, 2048], P(('tm', 'space'))
Inputs may be any that keep to these rules, and one draw needn't show every extreme that they name: Row b lists the key tiles of query block b, which lies in window w = b // 8 at block b % 8 of it. A value v names kv block v % 8 of window w - v // 8; windows below 0 are never named, nor, where v // 8 = 0, blocks at or after b % 8 except in slot 0. Slot 0 holds b % 8; slots 1 to u hold distinct other values, u from 0 to 5, ragged over the blocks; the remaining slots hold 0. Every draw has rows with u = 5 and names the largest value. `kinds`: kind 0: every key of the tile is visible; kind 1: a key is visible when its position in its tile is at most the query's position in its block; kind 2: the slot is unused. Slot 0 has kind 1, used slots kind 0 or 1, unused slots kind 2.
All inputs are finite; a program needn't handle non-finite values.
Results may differ from a plain program's by a relative error of at most 0.015.
Values may be sent and summed in bfloat16 or wider, within the bound.
A program may use at most 128 MiB of HBM per device.

v0:
```python
import math

import jax
import jax.numpy as jnp
from jax import lax
from jax.sharding import PartitionSpec as P

HEAD_SIZE = 128
BLOCK_TOKENS = 128
MAXT = 6
REACH = 2


def shifted_2(block, axis, distance):
    devices = range(lax.axis_size(axis))
    route = [(i - distance, i) for i in devices if i - distance in devices]
    return lax.ppermute(block, axis, route)


def block_grads(query_rows, grad_rows, key_tiles, value_tiles, tile_kinds):
    blocks, length, kv_count, head_dim = key_tiles.shape
    score_scale = 1.0 / head_dim**0.5
    key_flat = key_tiles.reshape(blocks * length, kv_count, head_dim)
    value_flat = value_tiles.reshape(blocks * length, kv_count, head_dim)
    scores = (
        jnp.einsum("qkgd,tkd->kgqt", query_rows, key_flat, preferred_element_type=jnp.float32)
        * score_scale
    )
    query_pos = jnp.arange(length)
    column_kind = jnp.repeat(tile_kinds, length)
    column_pos = jnp.tile(jnp.arange(length), blocks)
    visible = (column_kind == 0)[None, :] | (column_kind == 1)[None, :] & (
        column_pos[None, :] <= query_pos[:, None]
    )
    masked = jnp.where(visible, scores, -jnp.inf)
    row_max = jnp.max(masked, axis=-1, keepdims=True)
    weights = jnp.where(visible, jnp.exp(masked - row_max), 0.0)
    probabilities = weights / jnp.sum(weights, axis=-1, keepdims=True)
    probs_low = probabilities.astype(jnp.bfloat16)
    outputs = jnp.einsum(
        "kgqt,tkd->qkgd", probs_low, value_flat, preferred_element_type=jnp.float32
    )
    row_delta = jnp.einsum("qkgd,qkgd->kgq", grad_rows.astype(jnp.float32), outputs)
    grad_probs = jnp.einsum(
        "qkgd,tkd->kgqt", grad_rows, value_flat, preferred_element_type=jnp.float32
    )
    grad_scores = (score_scale * probabilities * (grad_probs - row_delta[..., None])).astype(
        jnp.bfloat16
    )
    grad_query = jnp.einsum(
        "kgqt,tkd->qkgd", grad_scores, key_flat, preferred_element_type=jnp.float32
    )
    grad_key = jnp.einsum(
        "kgqt,qkgd->tkd", grad_scores, query_rows, preferred_element_type=jnp.float32
    )
    grad_value = jnp.einsum(
        "kgqt,qkgd->tkd", probs_low, grad_rows, preferred_element_type=jnp.float32
    )
    return (
        grad_query.astype(jnp.bfloat16),
        grad_key.reshape(blocks, length, kv_count, head_dim),
        grad_value.reshape(blocks, length, kv_count, head_dim),
    )


def body(queries, keys, values, output_gradient, tiles, kinds):
    query_heads, grad_heads, key_heads, value_heads = (
        lax.all_to_all(queries, "space", split_axis=1, concat_axis=0, tiled=True),
        lax.all_to_all(output_gradient, "space", split_axis=1, concat_axis=0, tiled=True),
        lax.all_to_all(keys, "space", split_axis=1, concat_axis=0, tiled=True),
        lax.all_to_all(values, "space", split_axis=1, concat_axis=0, tiled=True),
    )
    window = query_heads.shape[0]
    kv_heads = key_heads.shape[1] // HEAD_SIZE
    head_groups = query_heads.shape[1] // key_heads.shape[1]
    per_window = window // BLOCK_TOKENS
    earlier = [shifted_2((key_heads, value_heads), "tm", offset) for offset in range(1, REACH + 1)]
    tile_count = (REACH + 1) * per_window
    key_tiles = jnp.concatenate([key_heads] + [shifted[0] for shifted in earlier], axis=0)
    key_tiles = key_tiles.reshape(tile_count, BLOCK_TOKENS, kv_heads, HEAD_SIZE)
    value_tiles = jnp.concatenate([value_heads] + [shifted[1] for shifted in earlier], axis=0)
    value_tiles = value_tiles.reshape(tile_count, BLOCK_TOKENS, kv_heads, HEAD_SIZE)
    group_size = math.gcd(per_window, 4)
    rounds = per_window // group_size
    query_groups = query_heads.reshape(
        rounds, group_size, BLOCK_TOKENS, kv_heads, head_groups, HEAD_SIZE
    )
    grad_groups = grad_heads.reshape(
        rounds, group_size, BLOCK_TOKENS, kv_heads, head_groups, HEAD_SIZE
    )
    tile_groups = tiles.reshape(rounds, group_size, MAXT)
    kind_groups = kinds.reshape(rounds, group_size, MAXT)

    def one_round(totals, inputs):
        summed_key_grad, summed_value_grad = totals
        query_part, grad_part, tile_part, kind_part = inputs
        flat_tiles = tile_part.reshape(group_size * MAXT)
        grad_query, grad_key, grad_value = jax.vmap(block_grads)(
            query_part, grad_part, key_tiles[tile_part], value_tiles[tile_part], kind_part
        )
        summed_key_grad = summed_key_grad.at[flat_tiles].add(
            grad_key.reshape(group_size * MAXT, BLOCK_TOKENS, kv_heads, HEAD_SIZE)
        )
        summed_value_grad = summed_value_grad.at[flat_tiles].add(
            grad_value.reshape(group_size * MAXT, BLOCK_TOKENS, kv_heads, HEAD_SIZE)
        )
        return ((summed_key_grad, summed_value_grad), grad_query)

    blank_total_sum = jnp.zeros((tile_count, BLOCK_TOKENS, kv_heads, HEAD_SIZE), jnp.float32)
    (summed_key_grad, summed_value_grad), grad_queries = lax.scan(
        one_round,
        (blank_total_sum, blank_total_sum),
        (query_groups, grad_groups, tile_groups, kind_groups),
    )
    key_parts = summed_key_grad.reshape(REACH + 1, window, kv_heads * HEAD_SIZE)
    value_parts = summed_value_grad.reshape(REACH + 1, window, kv_heads * HEAD_SIZE)
    key_total = key_parts[0]
    value_total = value_parts[0]
    for offset in range(1, REACH + 1):
        arrived = shifted_2((key_parts[offset], value_parts[offset]), "tm", -offset)
        key_total = key_total + arrived[0]
        value_total = value_total + arrived[1]
    grad_query_heads = grad_queries.reshape(window, head_groups * kv_heads * HEAD_SIZE)
    return (
        lax.all_to_all(grad_query_heads, "space", split_axis=0, concat_axis=1, tiled=True),
        lax.all_to_all(
            key_total.astype(jnp.bfloat16), "space", split_axis=0, concat_axis=1, tiled=True
        ),
        lax.all_to_all(
            value_total.astype(jnp.bfloat16), "space", split_axis=0, concat_axis=1, tiled=True
        ),
    )


def solution(mesh):
    in_specs = (
        P(("tm", "space"), None),
        P(("tm", "space"), None),
        P(("tm", "space"), None),
        P(("tm", "space"), None),
        P("tm", None),
        P("tm", None),
    )
    out_specs = (P(("tm", "space"), None), P(("tm", "space"), None), P(("tm", "space"), None))
    return jax.shard_map(body, mesh=mesh, in_specs=in_specs, out_specs=out_specs, check_vma=False)
```

profile of v0, /device:TPU:2, one launch (start us, length us, event | category | flops | bytes accessed | tf_op | source)
XLA Modules:
  0.0 453.6 jit_solution(1659445262904182512)
XLA Ops:
  3.1 11.5 %all-to-all-start.1 = ((bf16[128,8,256]{2,0,1:T(8,128)(2,1)}), bf16[128,8,256]{2,0,1:T(8,128)(2,1)S(1)}, u32[]{:S(2)}, u32[]{:S(2)}) async-start(bf16[128,8,256]{2,0,1:T(8,128)(2,1)} %copy.127), calls=%async_computation.1 | async-start | bytes 1048576 | tf_op jit(solution)/shard_map/all_to_all | solution.py:70
  15.8 11.3 %all-to-all-done.1 = bf16[128,8,256]{2,0,1:T(8,128)(2,1)S(1)} async-done(((bf16[128,8,256]{2,0,1:T(8,128)(2,1)}), bf16[128,8,256]{2,0,1:T(8,128)(2,1)S(1)}, u32[]{:S(2)}, u32[]{:S(2)}) %all-to-all-start.1) | async-done | bytes 524320 | tf_op jit(solution)/shard_map/all_to_all | solution.py:70
  27.1 6.9 %all-to-all-start.2 = ((bf16[128,8,256]{2,0,1:T(8,128)(2,1)}), bf16[128,8,256]{2,0,1:T(8,128)(2,1)S(1)}, u32[]{:S(2)}, u32[]{:S(2)}) async-start(bf16[128,8,256]{2,0,1:T(8,128)(2,1)} %copy.129), calls=%async_computation.2 | async-start | bytes 1048576 | tf_op jit(solution)/shard_map/all_to_all | solution.py:71
  35.3 8.9 %all-to-all-done.2 = bf16[128,8,256]{2,0,1:T(8,128)(2,1)S(1)} async-done(((bf16[128,8,256]{2,0,1:T(8,128)(2,1)}), bf16[128,8,256]{2,0,1:T(8,128)(2,1)S(1)}, u32[]{:S(2)}, u32[]{:S(2)}) %all-to-all-start.2) | async-done | bytes 524320 | tf_op jit(solution)/shard_map/all_to_all | solution.py:71
  44.3 9.6 %all-to-all-start = ((bf16[128,8,512]{0,2,1:T(8,128)(2,1)}), bf16[128,8,512]{0,2,1:T(8,128)(2,1)}, u32[]{:S(2)}, u32[]{:S(2)}) async-start(bf16[128,8,512]{0,2,1:T(8,128)(2,1)} %bitcast.31), calls=%async_computation | async-start | bytes 2097152 | tf_op jit(solution)/shard_map/all_to_all | solution.py:68
  53.9 2.3 copy.130
  56.1 12.2 %all-to-all-done = bf16[128,8,512]{0,2,1:T(8,128)(2,1)} async-done(((bf16[128,8,512]{0,2,1:T(8,128)(2,1)}), bf16[128,8,512]{0,2,1:T(8,128)(2,1)}, u32[]{:S(2)}, u32[]{:S(2)}) %all-to-all-start) | async-done | bytes 1048608 | tf_op jit(solution)/shard_map/all_to_all | solution.py:68
  68.4 8.3 %all-to-all-start.3 = ((bf16[128,8,512]{0,2,1:T(8,128)(2,1)}), bf16[128,8,512]{0,2,1:T(8,128)(2,1)}, u32[]{:S(2)}, u32[]{:S(2)}) async-start(bf16[128,8,512]{0,2,1:T(8,128)(2,1)} %bitcast.43), calls=%async_computation.3 | async-start | bytes 2097152 | tf_op jit(solution)/shard_map/all_to_all | solution.py:69
  78.0 15.4 %collective-permute-start.1 = (bf16[1024,256]{1,0:T(8,128)(2,1)S(1)}, bf16[1024,256]{1,0:T(8,128)(2,1)}, u32[]{:S(2)}, u32[]{:S(2)}) collective-permute-start(bf16[1024,256]{1,0:T(8,128)(2,1)S(1)} %bitcast.252), channel_id=1, source_target_pairs={{0,16},{8,24},{16,32},{24,40},{32,48},{40,56},{48,64},{56,72},{64,... | collective-permute-start | bytes 1572872 | tf_op jit(solution)/shard_map/ppermute | solution.py:17
  93.4 1.9 collective-permute-start.2
  95.3 2.2 collective-permute-start.3
  98.4 13.3 %collective-permute-done.1 = bf16[1024,256]{1,0:T(8,128)(2,1)} collective-permute-done((bf16[1024,256]{1,0:T(8,128)(2,1)S(1)}, bf16[1024,256]{1,0:T(8,128)(2,1)}, u32[]{:S(2)}, u32[]{:S(2)}) %collective-permute-start.1) | collective-permute-done | bytes 524320 | tf_op jit(solution)/shard_map/ppermute | solution.py:17
  113.0 1.9 reshape.184
  114.9 8.0 %collective-permute-done.3 = bf16[1024,256]{1,0:T(8,128)(2,1)} collective-permute-done((bf16[1024,256]{1,0:T(8,128)(2,1)S(1)}, bf16[1024,256]{1,0:T(8,128)(2,1)}, u32[]{:S(2)}, u32[]{:S(2)}) %collective-permute-start.3) | collective-permute-done | bytes 524320 | tf_op jit(solution)/shard_map/ppermute | solution.py:17
  124.0 1.9 reshape.185
  125.9 2.0 broadcast_in_dim.38
  128.0 2.0 broadcast_in_dim.38.clone
  130.0 181.7 %while.14 = (s32[]{:T(128)}, f32[24,128,2,128]{3,1,2,0:T(8,128)}, f32[24,128,2,128]{3,1,2,0:T(8,128)}, bf16[2,4,128,2,2,128]{2,5,4,3,1,0:T(8,128)(2,1)}, s32[2,4...) while((s32[]{:T(128)}, f32[24,128,2,128]{3,1,2,0:T(8,128)}, ...), condition=%wide.region_5.6_spmd, body=%wide.region_0.5_spmd.sunk | while | flops 2441445376 | bytes 197145456 | solution.py:110
  132.9 6.8 %gather_fusion.1 = bf16[24,128,2,128]{3,2,1,0:T(2,128)(2,1)S(1)} fusion(bf16[24,128,2,128]{3,2,1,0:T(2,128)(2,1)} %get-tuple-element.252, s32[1024]{0:T(1024)S(1)} %pad_clamp_fusion.2), kind=kCustom, calls=%fused_computation.clone.1 | custom fusion | bytes 3145824 | tf_op jit(solution)/shard_map/while/body/eval_jaxpr/gather | solution.py:99
  140.8 2.5 fusion.71
  143.3 3.3 fusion.72
  149.2 7.4 %gather_fusion = bf16[24,128,2,128]{3,2,1,0:T(2,128)(2,1)} fusion(bf16[24,128,2,128]{3,2,1,0:T(2,128)(2,1)} %get-tuple-element.253, s32[1024]{0:T(1024)S(1)} %pad_clamp_fusion.2), kind=kCustom, calls=%fused_computation.1.clone.1 | custom fusion | bytes 3145824 | tf_op jit(solution)/shard_map/while/body/eval_jaxpr/gather | solution.py:99
  156.6 5.0 %copy.211 = bf16[4,768,2,128,1]{1,3,4,2,0:T(8,128)(2,1)} copy(bf16[4,768,2,128,1]{3,2,1,0,4:T(2,128)(2,1)} %bitcast.236) | data formatting | bytes 3145728 | tf_op jit(solution)/shard_map/while/body/eval_jaxpr/vmap()/reshape | solution.py:24
  161.6 1.9 constant_dynamic-slice_fusion.4
  163.5 2.0 copy.209
  165.5 2.2 bitcast_convert_fusion.2
  167.7 2.5 copy.210
  170.2 2.6 fusion.74
  172.8 4.3 fusion.75
  178.8 3.9 convolution_bitcast_fusion.5
  182.7 3.6 copy.215
  186.2 3.9 copy.216
  190.2 9.4 %scatter_fusion = f32[24,128,2,128]{3,1,2,0:T(8,128)} fusion(f32[24,128,2,128]{3,1,2,0:T(8,128)} %get-tuple-element.235, s32[24]{0:T(128)S(1)} %fusion.70, f32[24,128,2,128]{3,1,2,0:T(8,128)} %copy.216), kind=kCustom, calls=%fused_computation.2.clone.1 | custom fusion | flops 786432 | bytes 9437280 | tf_op jit(solution)/shard_map/while/body/eval_jaxpr/scatter-add | solution.py:101
  199.6 3.9 convolution_bitcast_fusion.6
  203.5 2.4 copy.217
  207.7 9.8 %scatter_fusion.1 = f32[24,128,2,128]{3,1,2,0:T(8,128)} fusion(f32[24,128,2,128]{3,1,2,0:T(8,128)} %get-tuple-element.236, s32[24]{0:T(128)S(1)} %fusion.70, f32[24,128,2,128]{3,1,2,0:T(8,128)} %copy.218), kind=kCustom, calls=%fused_computation.3.clone.1 | custom fusion | flops 786432 | bytes 9437280 | tf_op jit(solution)/shard_map/while/body/eval_jaxpr/scatter-add | solution.py:104
  217.5 2.6 fusion.76
  224.0 6.8 %gather_fusion.1 = bf16[24,128,2,128]{3,2,1,0:T(2,128)(2,1)S(1)} fusion(bf16[24,128,2,128]{3,2,1,0:T(2,128)(2,1)} %get-tuple-element.252, s32[1024]{0:T(1024)S(1)} %pad_clamp_fusion.2), kind=kCustom, calls=%fused_computation.clone.1 | custom fusion | bytes 3145824 | tf_op jit(solution)/shard_map/while/body/eval_jaxpr/gather | solution.py:99
  231.9 2.5 fusion.71
  234.4 3.3 fusion.72
  240.4 7.4 %gather_fusion = bf16[24,128,2,128]{3,2,1,0:T(2,128)(2,1)} fusion(bf16[24,128,2,128]{3,2,1,0:T(2,128)(2,1)} %get-tuple-element.253, s32[1024]{0:T(1024)S(1)} %pad_clamp_fusion.2), kind=kCustom, calls=%fused_computation.1.clone.1 | custom fusion | bytes 3145824 | tf_op jit(solution)/shard_map/while/body/eval_jaxpr/gather | solution.py:99
  247.7 5.0 %copy.211 = bf16[4,768,2,128,1]{1,3,4,2,0:T(8,128)(2,1)} copy(bf16[4,768,2,128,1]{3,2,1,0,4:T(2,128)(2,1)} %bitcast.236) | data formatting | bytes 3145728 | tf_op jit(solution)/shard_map/while/body/eval_jaxpr/vmap()/reshape | solution.py:24
  254.6 2.0 copy.209
  256.6 2.2 bitcast_convert_fusion.2
  258.8 2.5 copy.210
  261.3 2.6 fusion.74
  264.0 4.3 fusion.75
  269.9 3.9 convolution_bitcast_fusion.5
  273.8 3.6 copy.215
  277.4 3.9 copy.216
  281.4 9.2 %scatter_fusion = f32[24,128,2,128]{3,1,2,0:T(8,128)} fusion(f32[24,128,2,128]{3,1,2,0:T(8,128)} %get-tuple-element.235, s32[24]{0:T(128)S(1)} %fusion.70, f32[24,128,2,128]{3,1,2,0:T(8,128)} %copy.216), kind=kCustom, calls=%fused_computation.2.clone.1 | custom fusion | flops 786432 | bytes 9437280 | tf_op jit(solution)/shard_map/while/body/eval_jaxpr/scatter-add | solution.py:101
  290.6 3.9 convolution_bitcast_fusion.6
  294.4 2.4 copy.217
  298.7 9.4 %scatter_fusion.1 = f32[24,128,2,128]{3,1,2,0:T(8,128)} fusion(f32[24,128,2,128]{3,1,2,0:T(8,128)} %get-tuple-element.236, s32[24]{0:T(128)S(1)} %fusion.70, f32[24,128,2,128]{3,1,2,0:T(8,128)} %copy.218), kind=kCustom, calls=%fused_computation.3.clone.1 | custom fusion | flops 786432 | bytes 9437280 | tf_op jit(solution)/shard_map/while/body/eval_jaxpr/scatter-add | solution.py:104
  308.1 2.6 fusion.76
  311.7 2.5 copy.174
  314.2 5.8 %all-to-all-start.4 = ((bf16[8,128,512]{2,1,0:T(8,128)(2,1)}), bf16[8,128,512]{2,1,0:T(8,128)(2,1)}, u32[]{:S(2)}, u32[]{:S(2)}) async-start(bf16[8,128,512]{2,1,0:T(8,128)(2,1)} %copy.174), calls=%async_computation.4 | async-start | bytes 2097152 | tf_op jit(solution)/shard_map/all_to_all | solution.py:125
  320.0 4.7 %fusion.29 = (f32[8,128,2,128]{3,1,2,0:T(8,128)}, f32[8,128,2,128]{3,1,2,0:T(8,128)}, f32[8,128,2,128]{3,1,2,0:T(8,128)}, f32[8,128,2,128]{3,1,2,0:T(8,128)}, f3...) fusion(f32[24,128,2,128]{3,1,2,0:T(8,128)} %get-tuple-element.59, f32[24,128,2,128]{3,1,2,0:T(8,128)S(1)} %copy-done.5), kind=kLoop, calls=%fused_computation.64 | loop fusion | bytes 12582912 | tf_op jit(solution)/shard_map/slice | solution.py:118
  337.9 4.2 collective-permute-done.6
  342.2 55.6 %collective-permute-done.7 = f32[1024,256]{0,1:T(8,128)} collective-permute-done((f32[1024,256]{0,1:T(8,128)}, f32[1024,256]{0,1:T(8,128)}, u32[]{:S(2)}, u32[]{:S(2)}) %collective-permute-start.7) | collective-permute-done | bytes 1048608 | tf_op jit(solution)/shard_map/ppermute | solution.py:17
  400.6 9.6 %all-to-all-start.6 = ((bf16[8,128,256]{2,1,0:T(8,128)(2,1)}), bf16[8,128,256]{2,1,0:T(8,128)(2,1)S(1)}, u32[]{:S(2)}, u32[]{:S(2)}) async-start(bf16[8,128,256]{2,1,0:T(8,128)(2,1)} %bitcast.52), calls=%async_computation.6 | async-start | bytes 1048576 | tf_op jit(solution)/shard_map/all_to_all | solution.py:129
  410.7 18.7 %collective-permute-done.5 = f32[1024,256]{0,1:T(8,128)} collective-permute-done((f32[1024,256]{0,1:T(8,128)}, f32[1024,256]{0,1:T(8,128)}, u32[]{:S(2)}, u32[]{:S(2)}) %collective-permute-start.5) | collective-permute-done | bytes 1048608 | tf_op jit(solution)/shard_map/ppermute | solution.py:17
  432.2 9.9 %all-to-all-start.5 = ((bf16[8,128,256]{2,1,0:T(8,128)(2,1)}), bf16[8,128,256]{2,1,0:T(8,128)(2,1)S(1)}, u32[]{:S(2)}, u32[]{:S(2)}) async-start(bf16[8,128,256]{2,1,0:T(8,128)(2,1)} %bitcast.49), calls=%async_computation.5 | async-start | bytes 1048576 | tf_op jit(solution)/shard_map/all_to_all | solution.py:126
  446.4 5.9 %all-to-all-done.5 = bf16[8,128,256]{2,1,0:T(8,128)(2,1)S(1)} async-done(((bf16[8,128,256]{2,1,0:T(8,128)(2,1)}), bf16[8,128,256]{2,1,0:T(8,128)(2,1)S(1)}, u32[]{:S(2)}, u32[]{:S(2)}) %all-to-all-start.5) | async-done | bytes 524320 | tf_op jit(solution)/shard_map/all_to_all | solution.py:126
  (120 shorter events, 58.4 us)
Async XLA Ops:
  0.6 13.9 %copy-start.15 = (bf16[128,2048]{1,0:T(8,128)(2,1)S(1)}, bf16[128,2048]{1,0:T(8,128)(2,1)}, u32[]{:S(2)}) copy-start(bf16[128,2048]{1,0:T(8,128)(2,1)} %param.10) | copy-start | bytes 1572868
  0.6 33.4 %copy-start.12 = (bf16[128,4096]{1,0:T(8,128)(2,1)S(1)}, bf16[128,4096]{1,0:T(8,128)(2,1)}, u32[]{:S(2)}) copy-start(bf16[128,4096]{1,0:T(8,128)(2,1)} %param.8) | copy-start | bytes 3145732
  3.1 24.0 %all-to-all-start.1 = ((bf16[128,8,256]{2,0,1:T(8,128)(2,1)}), bf16[128,8,256]{2,0,1:T(8,128)(2,1)S(1)}, u32[]{:S(2)}, u32[]{:S(2)}) async-start(bf16[128,8,256]{2,0,1:T(8,128)(2,1)} %copy.127), calls=%async_computation.1 | async-start | bytes 1048576 | tf_op jit(solution)/shard_map/all_to_all | solution.py:70
  27.1 17.2 %all-to-all-start.2 = ((bf16[128,8,256]{2,0,1:T(8,128)(2,1)}), bf16[128,8,256]{2,0,1:T(8,128)(2,1)S(1)}, u32[]{:S(2)}, u32[]{:S(2)}) async-start(bf16[128,8,256]{2,0,1:T(8,128)(2,1)} %copy.129), calls=%async_computation.2 | async-start | bytes 1048576 | tf_op jit(solution)/shard_map/all_to_all | solution.py:71
  44.3 24.1 %all-to-all-start = ((bf16[128,8,512]{0,2,1:T(8,128)(2,1)}), bf16[128,8,512]{0,2,1:T(8,128)(2,1)}, u32[]{:S(2)}, u32[]{:S(2)}) async-start(bf16[128,8,512]{0,2,1:T(8,128)(2,1)} %bitcast.31), calls=%async_computation | async-start | bytes 2097152 | tf_op jit(solution)/shard_map/all_to_all | solution.py:68
  68.4 57.6 %all-to-all-start.3 = ((bf16[128,8,512]{0,2,1:T(8,128)(2,1)}), bf16[128,8,512]{0,2,1:T(8,128)(2,1)}, u32[]{:S(2)}, u32[]{:S(2)}) async-start(bf16[128,8,512]{0,2,1:T(8,128)(2,1)} %bitcast.43), calls=%async_computation.3 | async-start | bytes 2097152 | tf_op jit(solution)/shard_map/all_to_all | solution.py:69
  76.7 20.9 %collective-permute-start = (bf16[1024,256]{1,0:T(8,128)(2,1)S(1)}, bf16[1024,256]{1,0:T(8,128)(2,1)S(1)}, u32[]{:S(2)}, u32[]{:S(2)}) collective-permute-start(bf16[1024,256]{1,0:T(8,128)(2,1)S(1)} %bitcast.251), channel_id=1, source_target_pairs={{0,8},{8,16},{16,24},{24,32},{32,40},{40,48},{48,56},{56,64},{64,7... | collective-permute-start | bytes 1572872 | tf_op jit(solution)/shard_map/ppermute | solution.py:17
  78.0 33.7 %collective-permute-start.1 = (bf16[1024,256]{1,0:T(8,128)(2,1)S(1)}, bf16[1024,256]{1,0:T(8,128)(2,1)}, u32[]{:S(2)}, u32[]{:S(2)}) collective-permute-start(bf16[1024,256]{1,0:T(8,128)(2,1)S(1)} %bitcast.252), channel_id=1, source_target_pairs={{0,16},{8,24},{16,32},{24,40},{32,48},{40,56},{48,64},{56,72},{64,... | collective-permute-start | bytes 1572872 | tf_op jit(solution)/shard_map/ppermute | solution.py:17
  93.4 21.5 %collective-permute-start.2 = (bf16[1024,256]{1,0:T(8,128)(2,1)S(1)}, bf16[1024,256]{1,0:T(8,128)(2,1)S(1)}, u32[]{:S(2)}, u32[]{:S(2)}) collective-permute-start(bf16[1024,256]{1,0:T(8,128)(2,1)S(1)} %bitcast.254), channel_id=1, source_target_pairs={{0,8},{8,16},{16,24},{24,32},{32,40},{40,48},{48,56},{56,64},{64,7... | collective-permute-start | bytes 1572872 | tf_op jit(solution)/shard_map/ppermute | solution.py:17
  95.3 27.6 %collective-permute-start.3 = (bf16[1024,256]{1,0:T(8,128)(2,1)S(1)}, bf16[1024,256]{1,0:T(8,128)(2,1)}, u32[]{:S(2)}, u32[]{:S(2)}) collective-permute-start(bf16[1024,256]{1,0:T(8,128)(2,1)S(1)} %bitcast.255), channel_id=1, source_target_pairs={{0,16},{8,24},{16,32},{24,40},{32,48},{40,56},{48,64},{56,72},{64,... | collective-permute-start | bytes 1572872 | tf_op jit(solution)/shard_map/ppermute | solution.py:17
  97.6 0.8 copy-start.16
  140.8 2.5 copy-start
  146.6 2.6 copy-start.4
  170.2 2.6 copy-start.3
  170.2 2.6 copy-start.6
  177.2 1.6 copy-start.2
  207.7 9.8 %copy-start.1 = (bf16[4,768,2,128,1]{1,3,4,2,0:T(8,128)(2,1)S(1)}, bf16[4,768,2,128,1]{1,3,4,2,0:T(8,128)(2,1)}, u32[]{:S(2)}) copy-start(bf16[4,768,2,128,1]{1,3,4,2,0:T(8,128)(2,1)} %copy-done) | copy-start | bytes 4718596 | tf_op jit(solution)/shard_map/while
  207.7 9.8 %copy-start.13 = (bf16[2,4,128,2,2,128]{2,5,4,3,1,0:T(8,128)(2,1)S(1)}, bf16[2,4,128,2,2,128]{2,5,4,3,1,0:T(8,128)(2,1)}, u32[]{:S(2)}) copy-start(bf16[2,4,128,2,2,128]{2,5,4,3,1,0:T(8,128)(2,1)} %get-tuple-element.237) | copy-start | bytes 3145732 | tf_op jit(solution)/shard_map/while
  220.1 1.0 copy-start.14
  231.9 2.5 copy-start
  237.8 2.6 copy-start.4
  261.3 2.6 copy-start.3
  261.3 2.6 copy-start.6
  268.3 1.6 copy-start.2
  298.7 9.4 %copy-start.1 = (bf16[4,768,2,128,1]{1,3,4,2,0:T(8,128)(2,1)S(1)}, bf16[4,768,2,128,1]{1,3,4,2,0:T(8,128)(2,1)}, u32[]{:S(2)}) copy-start(bf16[4,768,2,128,1]{1,3,4,2,0:T(8,128)(2,1)} %copy-done) | copy-start | bytes 4718596 | tf_op jit(solution)/shard_map/while
  298.7 9.4 %copy-start.13 = (bf16[2,4,128,2,2,128]{2,5,4,3,1,0:T(8,128)(2,1)S(1)}, bf16[2,4,128,2,2,128]{2,5,4,3,1,0:T(8,128)(2,1)}, u32[]{:S(2)}) copy-start(bf16[2,4,128,2,2,128]{2,5,4,3,1,0:T(8,128)(2,1)} %get-tuple-element.237) | copy-start | bytes 3145732 | tf_op jit(solution)/shard_map/while
  310.7 1.0 copy-start.14
  311.7 8.3 %copy-start.5 = (f32[24,128,2,128]{3,1,2,0:T(8,128)S(1)}, f32[24,128,2,128]{3,1,2,0:T(8,128)}, u32[]{:S(2)}) copy-start(f32[24,128,2,128]{3,1,2,0:T(8,128)} %get-tuple-element.58) | copy-start | bytes 9437188
  314.2 86.5 %all-to-all-start.4 = ((bf16[8,128,512]{2,1,0:T(8,128)(2,1)}), bf16[8,128,512]{2,1,0:T(8,128)(2,1)}, u32[]{:S(2)}, u32[]{:S(2)}) async-start(bf16[8,128,512]{2,1,0:T(8,128)(2,1)} %copy.174), calls=%async_computation.4 | async-start | bytes 2097152 | tf_op jit(solution)/shard_map/all_to_all | solution.py:125
  324.7 4.2 copy-start.11
  326.4 5.4 %copy-start.10 = (f32[8,128,2,128]{3,1,2,0:T(8,128)S(1)}, f32[8,128,2,128]{3,1,2,0:T(8,128)}, u32[]{:S(2)}) copy-start(f32[8,128,2,128]{3,1,2,0:T(8,128)} %get-tuple-element.143) | copy-start | bytes 3145732
  327.6 14.6 %collective-permute-start.6 = (f32[1024,256]{0,1:T(8,128)}, f32[1024,256]{0,1:T(8,128)}, u32[]{:S(2)}, u32[]{:S(2)}) collective-permute-start(f32[1024,256]{0,1:T(8,128)} %bitcast.171), channel_id=1, source_target_pairs={{8,0},{16,8},{24,16},{32,24},{40,32},{48,40},{56,48},{64,56},{72,6... | collective-permute-start | bytes 3145736 | tf_op jit(solution)/shard_map/ppermute | solution.py:17
  329.3 5.3 %copy-start.9 = (f32[8,128,2,128]{3,1,2,0:T(8,128)S(1)}, f32[8,128,2,128]{3,1,2,0:T(8,128)}, u32[]{:S(2)}) copy-start(f32[8,128,2,128]{3,1,2,0:T(8,128)} %get-tuple-element.144) | copy-start | bytes 3145732
  330.4 67.3 %collective-permute-start.7 = (f32[1024,256]{0,1:T(8,128)}, f32[1024,256]{0,1:T(8,128)}, u32[]{:S(2)}, u32[]{:S(2)}) collective-permute-start(f32[1024,256]{0,1:T(8,128)} %bitcast.170), channel_id=1, source_target_pairs={{16,0},{24,8},{32,16},{40,24},{48,32},{56,40},{64,48},{72,56},{80,... | collective-permute-start | bytes 3145736 | tf_op jit(solution)/shard_map/ppermute | solution.py:17
  332.1 5.4 %copy-start.8 = (f32[8,128,2,128]{3,1,2,0:T(8,128)S(1)}, f32[8,128,2,128]{3,1,2,0:T(8,128)}, u32[]{:S(2)}) copy-start(f32[8,128,2,128]{3,1,2,0:T(8,128)} %get-tuple-element.137) | copy-start | bytes 3145732
  333.3 77.3 %collective-permute-start.4 = (f32[1024,256]{0,1:T(8,128)}, f32[1024,256]{0,1:T(8,128)}, u32[]{:S(2)}, u32[]{:S(2)}) collective-permute-start(f32[1024,256]{0,1:T(8,128)} %bitcast.173), channel_id=1, source_target_pairs={{8,0},{16,8},{24,16},{32,24},{40,32},{48,40},{56,48},{64,56},{72,6... | collective-permute-start | bytes 3145736 | tf_op jit(solution)/shard_map/ppermute | solution.py:17
  336.2 93.2 %collective-permute-start.5 = (f32[1024,256]{0,1:T(8,128)}, f32[1024,256]{0,1:T(8,128)}, u32[]{:S(2)}, u32[]{:S(2)}) collective-permute-start(f32[1024,256]{0,1:T(8,128)} %bitcast.172), channel_id=1, source_target_pairs={{16,0},{24,8},{32,16},{40,24},{48,32},{56,40},{64,48},{72,56},{80,... | collective-permute-start | bytes 3145736 | tf_op jit(solution)/shard_map/ppermute | solution.py:17
  337.9 72.3 %copy-start.7 = (f32[8,128,2,128]{3,1,2,0:T(8,128)S(1)}, f32[8,128,2,128]{3,1,2,0:T(8,128)}, u32[]{:S(2)}) copy-start(f32[8,128,2,128]{3,1,2,0:T(8,128)} %get-tuple-element.145) | copy-start | bytes 3145732
  400.6 31.6 %all-to-all-start.6 = ((bf16[8,128,256]{2,1,0:T(8,128)(2,1)}), bf16[8,128,256]{2,1,0:T(8,128)(2,1)S(1)}, u32[]{:S(2)}, u32[]{:S(2)}) async-start(bf16[8,128,256]{2,1,0:T(8,128)(2,1)} %bitcast.52), calls=%async_computation.6 | async-start | bytes 1048576 | tf_op jit(solution)/shard_map/all_to_all | solution.py:129
  432.2 20.1 %all-to-all-start.5 = ((bf16[8,128,256]{2,1,0:T(8,128)(2,1)}), bf16[8,128,256]{2,1,0:T(8,128)(2,1)S(1)}, u32[]{:S(2)}, u32[]{:S(2)}) async-start(bf16[8,128,256]{2,1,0:T(8,128)(2,1)} %bitcast.49), calls=%async_computation.5 | async-start | bytes 1048576 | tf_op jit(solution)/shard_map/all_to_all | solution.py:126
where the time goes:
time: 463 us; the launch traced here: 454 us
  waiting for transfers between devices  138 us (30%)
  local copies, waits for them, and re-layouts  125 us (27%)
  starting transfers between devices  87.7 us (19%)
  other arithmetic  61.8 us (13%)
  matrix products  39.5 us (9%)
    ppermute x8, waiting for transfers between devices, shifted_2(): return lax.ppermute(block, axis, route)  99.9 us
    ppermute x8, starting transfers between devices, shifted_2(): return lax.ppermute(block, axis, route)  26 us
    scatter-add x2, other arithmetic, one_round(): summed_value_grad.at[flat_tiles]  19.2 us
    scatter-add x2, other arithmetic, one_round(): summed_key_grad.at[flat_tiles]  18.6 us
    gather x2, local copies, waits for them, and re-layouts, one_round(): value_tiles[tile_part]  14.8 us
    while x40, local copies, waits for them, and re-layouts  14.2 us
    unnamed x29, local copies, waits for them, and re-layouts  14.1 us
    gather x2, local copies, waits for them, and re-layouts, one_round(): key_tiles[tile_part]  13.6 us
  transfers between devices with their start and end apart: 15, of which 9 were waited for; matrix products, arithmetic and copies ran while one was open for 7% of the time, Pallas kernels for 0%

commit v1 on v0

v1 whole, which is shorter than its diff:
```python
import functools

import jax
import jax.numpy as jnp
from jax import lax
from jax.experimental import pallas as pl
from jax.experimental.pallas import tpu as pltpu
from jax.sharding import PartitionSpec as P

HEAD = 128
BLOCK = 128
MAXT = 6
HEADS = 4
UNITS = 2 * HEADS
TILES = 24
PLUS = (1, 4, 6)
MINUS = (0, 2, 3, 5, 7)
X_ORDER = (0, 1, 2, 4, 3, 6, 5, 7)
MESH = pl.DeviceIdType.MESH
LOG2E = 1.4426950408889634


def place():
    tm = lax.axis_index("tm")
    space = lax.axis_index("space")
    core = lax.rem(tm, 2)
    z_lo = lax.rem(lax.div(tm, 2), 4)
    x = lax.rem(space, 4)
    z_hi = lax.div(space, 4)
    return tm, core, x, z_hi, z_hi * 4 + z_lo


def ring_peers():
    tm, core, x, z_hi, z = place()

    def at(tm_step, z_step):
        there = lax.rem(z + z_step, 8)
        return {"tm": lax.rem(tm + tm_step, 32), "space": lax.div(there, 4) * 4 + x}

    right, left, far_right, far_left = at(2, 1), at(30, 7), at(2, 5), at(30, 3)
    partner = {"tm": tm + 1 - 2 * core, "space": z_hi * 4 + x}
    along_x = [{"tm": tm, "space": z_hi * 4 + lax.rem(x + d, 4)} for d in (1, 2, 3)]
    return right, left, far_right, far_left, partner, along_x


def meet(peers):
    barrier = pltpu.get_barrier_semaphore()
    for peer in peers:
        pl.semaphore_signal(barrier, inc=1, device_id=peer, device_id_type=MESH)
    pl.semaphore_wait(barrier, len(peers))


def send(src, dst, sems, index, device):
    send_sem, recv_sem = sems
    copy = pltpu.make_async_remote_copy(
        src_ref=src,
        dst_ref=dst,
        send_sem=send_sem.at[index],
        recv_sem=recv_sem.at[index],
        device_id=device,
        device_id_type=MESH,
    )
    copy.start()
    return copy


def columns(start, width):
    return pl.ds(pl.multiple_of(start, width), width)


def gather_kernel(
    q_ref, k_ref, v_ref, g_ref, kv_ref, qh_ref, gh_ref,
    xs, xr, qs, qr, s1, r1, s2, r2, s3, r3, sp, rp, local,
):
    tm, core, x, z_hi, z = place()
    right, left, far_right, far_left, partner, along_x = ring_peers()
    from_left = lax.div(lax.rem(z + 7, 8), 4)
    from_far = 1 - from_left
    opposite = 1 - z_hi
    meet([right, left, far_right, far_left, partner] + along_x)

    def quad(window, half):
        return pl.ds(window * 8 + half * 4, 4)

    def source(unit, to_x):
        ref = v_ref if unit % 2 else k_ref
        return ref.at[:, columns((to_x * HEADS + unit // 2) * HEAD, HEAD)]

    waits = []
    x_copies = {}
    own_copies = {}
    for unit in X_ORDER:
        x_copies[unit] = [
            send(source(unit, lax.rem(x + d, 4)), kv_ref.at[unit, z_hi * 4 + x],
                 (xs, xr), unit * 3 + d - 1, along_x[d - 1])
            for d in (1, 2, 3)
        ]
        own = pltpu.make_async_copy(source(unit, x), kv_ref.at[unit, z_hi * 4 + x], local.at[unit])
        own.start()
        own_copies[unit] = own
        waits += x_copies[unit]
    q_copies = []
    for i, (ref, to) in enumerate(((q_ref, qh_ref), (g_ref, gh_ref))):
        for d in (1, 2, 3):
            q_copies.append(
                send(ref.at[:, columns(lax.rem(x + d, 4) * 1024, 1024)], to.at[x],
                     (qs, qr), i * 3 + d - 1, along_x[d - 1])
            )
        own = pltpu.make_async_copy(ref.at[:, columns(x * 1024, 1024)], to.at[x], local.at[UNITS + i])
        own.start()
        own_copies[UNITS + i] = own
    waits += q_copies

    first, second, third = {}, {}, {}

    def to_right(unit):
        piece = kv_ref.at[unit, quad(0, z_hi)]
        first[unit] = send(piece, kv_ref.at[unit, quad(2, z_hi)], (s1, r1), unit, right)

    for unit in X_ORDER:
        own_copies[unit].wait()
        for copy in x_copies[unit]:
            copy.wait_recv()
        if unit in PLUS:
            to_right(unit)
        else:
            piece = kv_ref.at[unit, quad(0, z_hi)]
            second[unit] = send(piece, kv_ref.at[unit, quad(2, z_hi)], (s2, r2), unit, far_right)
    for unit in PLUS:
        first[unit].wait_recv()
        piece = kv_ref.at[unit, quad(2, from_left)]
        second[unit] = send(piece, kv_ref.at[unit, quad(0, from_left)], (s2, r2), unit, far_left)
    for unit in MINUS:
        to_right(unit)

    def to_partner(unit):
        piece = kv_ref.at[unit, pl.ds(core * 16, 8)]
        return send(piece, kv_ref.at[unit, pl.ds(8, 8)], (sp, rp), unit, partner)

    across = []
    for unit in MINUS:
        second[unit].wait_recv()
        piece = kv_ref.at[unit, quad(2, from_far)]
        third[unit] = send(piece, kv_ref.at[unit, quad(0, from_far)], (s3, r3), unit, left)
    for unit in PLUS:
        second[unit].wait_recv()
        piece = kv_ref.at[unit, quad(0, opposite)]
        third[unit] = send(piece, kv_ref.at[unit, quad(2, opposite)], (s3, r3), unit, right)
    for unit in MINUS:
        first[unit].wait_recv()
        third[unit].wait_recv()
        across.append(to_partner(unit))
    for unit in PLUS:
        third[unit].wait_recv()
        across.append(to_partner(unit))
    for copy in q_copies + across:
        copy.wait_recv()
    own_copies[UNITS].wait()
    own_copies[UNITS + 1].wait()
    for table in (first, second, third):
        waits += list(table.values())
    for copy in waits + across:
        copy.wait_send()


def gather(queries, keys, values, grads):
    spec = pl.BlockSpec(memory_space=pltpu.VMEM)
    dma = pltpu.SemaphoreType.DMA
    return pl.pallas_call(
        gather_kernel,
        name="gather_heads",
        out_shape=(
            jax.ShapeDtypeStruct((UNITS, TILES, BLOCK, HEAD), jnp.bfloat16),
            jax.ShapeDtypeStruct((4, BLOCK, 1024), jnp.bfloat16),
            jax.ShapeDtypeStruct((4, BLOCK, 1024), jnp.bfloat16),
        ),
        in_specs=[spec] * 4,
        out_specs=(spec,) * 3,
        scratch_shapes=[dma((24,)), dma((24,)), dma((6,)), dma((6,))]
        + [dma((UNITS,))] * 8
        + [dma((UNITS + 2,))],
        compiler_params=pltpu.CompilerParams(
            collective_id=1, has_side_effects=True, vmem_limit_bytes=24 << 20
        ),
    )(queries, keys, values, grads)


NT = (((1,), (1,)), ((), ()))
NN = (((1,), (0,)), ((), ()))
TN = (((0,), (0,)), ((), ()))


def dot(a, b, dims):
    return lax.dot_general(a, b, dims, preferred_element_type=jnp.float32)


def grads_kernel(tiles_ref, kinds_ref, kv_ref, q_ref, g_ref, dkv_ref, dq_ref, acc):
    scale = 1.0 / HEAD**0.5
    half = lax.div(lax.axis_index("space"), 4)
    acc[...] = jnp.zeros_like(acc)
    row = lax.broadcasted_iota(jnp.int32, (BLOCK, 2 * BLOCK), 0)
    col = lax.broadcasted_iota(jnp.int32, (BLOCK, 2 * BLOCK), 1)
    ahead = row - jnp.where(col >= BLOCK, col - BLOCK, col)
    for b in range(4):
        line = half * 4 + b
        names = [tiles_ref[line, m] for m in range(MAXT)]
        kinds = [kinds_ref[line, m] for m in range(MAXT)]
        k = jnp.concatenate([kv_ref[0, t] for t in names], axis=0)
        v = jnp.concatenate([kv_ref[1, t] for t in names], axis=0)
        q = jnp.concatenate([q_ref[b, :, :HEAD], q_ref[b, :, HEAD:]], axis=0)
        g = jnp.concatenate([g_ref[b, :, :HEAD], g_ref[b, :, HEAD:]], axis=0)
        scores = dot(k, q, NT)
        masked = []
        for m in range(MAXT):
            limit = jnp.where(kinds[m] == 0, BLOCK, jnp.where(kinds[m] == 1, 0, -2 * BLOCK))
            masked.append(
                jnp.where(ahead <= limit, scores[m * BLOCK : (m + 1) * BLOCK], -jnp.inf)
            )
        scores = jnp.concatenate(masked, axis=0)
        top = jnp.max(scores, axis=0, keepdims=True)
        weights = jnp.exp2((scores - top) * (scale * LOG2E))
        probs = weights * (1.0 / jnp.sum(weights, axis=0, keepdims=True))
        low = probs.astype(jnp.bfloat16)
        grad_probs = dot(v, g, NT)
        delta = jnp.sum(low.astype(jnp.float32) * grad_probs, axis=0, keepdims=True)
        grad_scores = (probs * (grad_probs - delta) * scale).astype(jnp.bfloat16)
        grad_values = dot(low, g, NN)
        grad_keys = dot(grad_scores, q, NN)
        grad_q = dot(grad_scores, k, TN).astype(jnp.bfloat16)
        dq_ref[b, :, :HEAD] = grad_q[:BLOCK]
        dq_ref[b, :, HEAD:] = grad_q[BLOCK:]
        for m in range(MAXT):
            rows = slice(m * BLOCK, (m + 1) * BLOCK)
            acc[0, names[m]] += grad_keys[rows]
            acc[1, names[m]] += grad_values[rows]
    dkv_ref[...] = acc[...].astype(jnp.bfloat16)


def local_grads(tiles, kinds, kv, qh, gh):
    pair = pl.BlockSpec((2, TILES, BLOCK, HEAD), lambda h, *_: (h, 0, 0, 0))
    heads = pl.BlockSpec((4, BLOCK, 2 * HEAD), lambda h, *_: (0, 0, h))
    return pl.pallas_call(
        grads_kernel,
        name="local_grads",
        out_shape=(
            jax.ShapeDtypeStruct((UNITS, TILES, BLOCK, HEAD), jnp.bfloat16),
            jax.ShapeDtypeStruct((4, BLOCK, 1024), jnp.bfloat16),
        ),
        grid_spec=pltpu.PrefetchScalarGridSpec(
            num_scalar_prefetch=2,
            grid=(HEADS,),
            in_specs=[pair, heads, heads],
            out_specs=(pair, heads),
            scratch_shapes=[pltpu.VMEM((2, TILES, BLOCK, HEAD), jnp.float32)],
        ),
        compiler_params=pltpu.CompilerParams(vmem_limit_bytes=32 << 20),
    )(tiles, kinds, kv, qh, gh)


def scatter_kernel(
    dkv_ref, dq_ref, oq_ref, ok_ref, ov_ref,
    part, near, mid, back, summed, relay, total,
    xs, xr, qs, qr, s1, r1, s2, r2, s3, r3, sp, rp, local,
):
    tm, core, x, z_hi, z = place()
    right, left, far_right, far_left, partner, along_x = ring_peers()
    from_left = lax.div(lax.rem(z + 7, 8), 4)
    from_far = 1 - from_left
    opposite = 1 - z_hi
    meet([right, left, far_right, far_left, partner] + along_x)
    order = X_ORDER
    f32, bf16 = jnp.float32, jnp.bfloat16

    waits = []
    across = {}
    for unit in order:
        across[unit] = send(dkv_ref.at[unit, pl.ds(8, 8)], part.at[unit], (sp, rp), unit, partner)
    q_copies = []
    for d in (1, 2, 3):
        q_copies.append(
            send(dq_ref.at[lax.rem(x + d, 4)], oq_ref.at[:, columns(x * 1024, 1024)],
                 (qs, qr), d - 1, along_x[d - 1])
        )
    own_q = pltpu.make_async_copy(
        dq_ref.at[x], oq_ref.at[:, columns(x * 1024, 1024)], local.at[UNITS]
    )
    own_q.start()

    def quad(kept, half):
        return pl.ds(kept * 8 + half * 4, 4)

    def add(*terms):
        out = terms[0].astype(f32)
        for term in terms[1:]:
            out = out + term.astype(f32)
        return out.astype(bf16)

    first, second, third = {}, {}, {}
    for unit in order:
        across[unit].wait_recv()
        summed[unit, pl.ds(core * 8, 8)] = add(dkv_ref[unit, pl.ds(core * 16, 8)], part[unit])
        summed[unit, pl.ds(8 - core * 8, 8)] = dkv_ref[unit, pl.ds(16 - core * 16, 8)]
        if unit in PLUS:
            piece = summed.at[unit, quad(1, from_far)]
            first[unit] = send(piece, near.at[unit], (s1, r1), unit, left)
        else:
            piece = summed.at[unit, quad(0, opposite)]
            first[unit] = send(piece, near.at[unit], (s1, r1), unit, right)
    for unit in order:
        first[unit].wait_recv()
        if unit in PLUS:
            relay[unit] = add(near[unit], summed[unit, quad(0, opposite)])
            second[unit] = send(relay.at[unit], mid.at[unit], (s2, r2), unit, far_right)
        else:
            relay[unit] = add(near[unit], summed[unit, quad(1, from_far)])
            second[unit] = send(relay.at[unit], mid.at[unit], (s2, r2), unit, far_left)
            piece = summed.at[unit, quad(1, from_left)]
            third[unit] = send(piece, back.at[unit], (s3, r3), unit, left)
    passed = {}
    for unit in PLUS:
        second[unit].wait_recv()
        first[unit].wait_send()
        total[unit] = add(mid[unit], summed[unit, quad(1, from_left)])
        third[unit] = send(total.at[unit], back.at[unit], (s3, r3), unit, left)

    x_copies = []

    def finish(unit):
        third[unit].wait_recv()
        if unit in PLUS:
            third[unit].wait_send()
            total[unit] = add(summed[unit, quad(0, z_hi)], back[unit])
        else:
            second[unit].wait_recv()
            total[unit] = add(summed[unit, quad(0, z_hi)], mid[unit], back[unit])
        ref = ov_ref if unit % 2 else ok_ref
        place_there = columns((x * HEADS + unit // 2) * HEAD, HEAD)
        for d in (1, 2, 3):
            x_copies.append(
                send(total.at[unit, lax.rem(x + d, 4)], ref.at[:, place_there],
                     (xs, xr), unit * 3 + d - 1, along_x[d - 1])
            )
        own = pltpu.make_async_copy(total.at[unit, x], ref.at[:, place_there], local.at[unit])
        own.start()
        return own

    owns = [own_q] + [finish(unit) for unit in MINUS + PLUS]
    for copy in q_copies + x_copies:
        copy.wait_recv()
    for own in owns:
        own.wait()
    for unit in range(UNITS):
        across[unit].wait_send()
        second[unit].wait_send()
        if unit not in PLUS:
            first[unit].wait_send()
            third[unit].wait_send()
    for copy in q_copies + x_copies:
        copy.wait_send()


def scatter(dkv, dq):
    spec = pl.BlockSpec(memory_space=pltpu.VMEM)
    dma = pltpu.SemaphoreType.DMA
    unit = pltpu.VMEM((UNITS, 4, BLOCK, HEAD), jnp.bfloat16)
    return pl.pallas_call(
        scatter_kernel,
        name="scatter_heads",
        out_shape=(
            jax.ShapeDtypeStruct((BLOCK, 4096), jnp.bfloat16),
            jax.ShapeDtypeStruct((BLOCK, 2048), jnp.bfloat16),
            jax.ShapeDtypeStruct((BLOCK, 2048), jnp.bfloat16),
        ),
        in_specs=[spec] * 2,
        out_specs=(spec,) * 3,
        scratch_shapes=[
            pltpu.VMEM((UNITS, 8, BLOCK, HEAD), jnp.bfloat16),
            unit,
            unit,
            unit,
            pltpu.VMEM((UNITS, 16, BLOCK, HEAD), jnp.bfloat16),
            unit,
            unit,
        ]
        + [dma((24,)), dma((24,)), dma((3,)), dma((3,))]
        + [dma((UNITS,))] * 8
        + [dma((UNITS + 1,))],
        compiler_params=pltpu.CompilerParams(
            collective_id=2, has_side_effects=True, vmem_limit_bytes=32 << 20
        ),
    )(dkv, dq)


def body(queries, keys, values, output_gradient, tiles, kinds):
    kv, qh, gh = gather(queries, keys, values, output_gradient)
    dkv, dq = local_grads(tiles, kinds, kv, qh, gh)
    return scatter(dkv, dq)


def solution(mesh):
    rows = P(("tm", "space"), None)
    return jax.shard_map(
        body,
        mesh=mesh,
        in_specs=(rows, rows, rows, rows, P("tm", None), P("tm", None)),
        out_specs=(rows, rows, rows),
        check_vma=False,
    )
```

time: 463 us -> 179 us (0.39); the launches traced: 454 us -> 179 us
  Pallas kernels: 0 us -> 170 us
  waiting for transfers between devices: 138 us -> 0 us
  local copies, waits for them, and re-layouts: 125 us -> 8.45 us
  starting transfers between devices: 87.7 us -> 0 us
  other arithmetic: 61.8 us -> 0 us
  matrix products: 39.5 us -> 0 us
    pallas_call x0 -> x3, Pallas kernels: none -> 170 us  [the longest x1 76.6 us: gather(): pl.pallas_call(gather_kernel, name='gather_heads', out_shape=(jax.ShapeDt...]
    ppermute x8 -> x0, waiting for transfers between devices: 99.9 us -> none  [shifted_2(): return lax.ppermute(block, axis, route)]
    all_to_all x7 -> x0, starting transfers between devices: 61.7 us -> none  [the longest x1 11.5 us: body(): lax.all_to_all(keys, 'space', split_axis=1, concat_axis=0, tiled=True)]
    dot_general x12 -> x0, matrix products: 39.5 us -> none  [the longest x2 8.65 us: block_grads(): jnp.einsum('qkgd,tkd->kgqt', grad_rows, value_flat, preferred_element_typ...]
    all_to_all x7 -> x0, waiting for transfers between devices: 38.3 us -> none  [the longest x1 12.2 us: body(): lax.all_to_all(queries, 'space', split_axis=1, concat_axis=0, tiled=True)]
    scatter-add x4 -> x0, other arithmetic: 37.7 us -> none  [the longest x2 19.2 us: one_round(): summed_value_grad.at[flat_tiles]]
    gather x4 -> x0, local copies, waits for them, and re-layouts: 28.3 us -> none  [the longest x2 14.8 us: one_round(): value_tiles[tile_part]]
    reshape x12 -> x0, local copies, waits for them, and re-layouts: 27.6 us -> none  [the longest x2 9.91 us: block_grads(): value_flat = value_tiles.reshape(blocks * length, kv_count, head_dim)]
  transfers between devices with their start and end apart: 15 -> 0, of which waited for: 9 -> 0; matrix products, arithmetic and copies ran while one was open for 7% -> 0% of each run, Pallas kernels for 0% -> 0%
where the time goes in v1:
time: 179 us
  Pallas kernels  170 us (95%)
  local copies, waits for them, and re-layouts  8.45 us (5%)
    pallas_call x1, Pallas kernels, gather(): pl.pallas_call(gather_kernel, name='gather_heads', out_shape=(jax.ShapeDt...  76.6 us
    pallas_call x1, Pallas kernels, scatter(): pl.pallas_call(scatter_kernel, name='scatter_heads', out_shape=(jax.Shape...  74.1 us
    pallas_call x1, Pallas kernels, local_grads(): pl.pallas_call(grads_kernel, name='local_grads', out_shape=(jax.ShapeDtyp...  19.2 us
    unnamed x15, local copies, waits for them, and re-layouts  8.45 us

profile of v1, /device:TPU:2, one launch (start us, length us, event | category | flops | bytes accessed | tf_op | source)
XLA Modules:
  0.0 179.1 jit_solution(9555941406168393665)
XLA Ops:
  0.6 0.0 copy-start
  0.6 1.2 copy-done
  1.9 0.0 copy-start.1
  1.9 1.2 copy-done.1
  3.1 0.0 copy-start.2
  3.1 1.0 copy-done.2
  4.1 0.0 copy-start.3
  4.1 1.0 copy-done.3
  5.2 76.6 %gather_heads.1 = (bf16[8,24,128,128]{3,2,1,0:T(8,128)(2,1)S(1)}, bf16[4,128,1024]{2,1,0:T(8,128)(2,1)S(1)}, bf16[4,128,1024]{2,1,0:T(8,128)(2,1)S(1)}) custom-call(bf16[128,4096]{1,0:T(8,128)(2,1)S(1)} %copy-done, bf16[128,2048]{1,0:T(8,128)(2,1)S(1)} %copy-done.2, bf16[128,2048]{1,0:T(8,128)(2,1)S(1)} %copy-done.3, bf16[128,4096]{1,0:T(8,128)(2,1)S(1)} %copy-done.1), custom_call_target="tpu_custom_call" | custom-call | tf_op jit(solution)/shard_map/gather_heads/pallas_call | solution.py:169
  81.8 0.0 copy-start.4
  81.8 0.7 copy-done.4
  82.5 0.0 copy-start.5
  82.5 0.7 copy-done.5
  83.2 19.2 %local_grads.1 = (bf16[8,24,128,128]{3,2,1,0:T(8,128)(2,1)S(1)}, bf16[4,128,1024]{2,1,0:T(8,128)(2,1)S(1)}) custom-call(s32[8,6]{1,0:T(8,128)S(1)} %copy-done.4, s32[8,6]{1,0:T(8,128)S(1)} %copy-done.5, bf16[8,24,128,128]{3,2,1,0:T(8,128)(2,1)S(1)} %get-tuple-element.8.kv_ref, bf16[4,128,1024]{2,1,0:T(8,128)(2,1)S(1)} %get-tuple-element.9.q_ref, ...), custom_call_target="tpu_custom_call" | custom-call | tf_op jit(solution)/shard_map/local_grads/pallas_call | solution.py:242
  102.4 74.1 %scatter_heads.1 = (bf16[128,4096]{1,0:T(8,128)(2,1)S(1)}, bf16[128,2048]{1,0:T(8,128)(2,1)S(1)}, bf16[128,2048]{1,0:T(8,128)(2,1)S(1)}) custom-call(bf16[8,24,128,128]{3,2,1,0:T(8,128)(2,1)S(1)} %get-tuple-element.11.dkv_ref, bf16[4,128,1024]{2,1,0:T(8,128)(2,1)S(1)} %get-tuple-element.12.dq_ref), custom_call_target="tpu_custom_call" | custom-call | tf_op jit(solution)/shard_map/scatter_heads/pallas_call | solution.py:366
  176.6 1.0 copy.12
  177.5 0.8 copy.13
  178.3 0.8 copy.14
Async XLA Ops:
  0.6 1.2 copy-start
  1.9 1.2 copy-start.1
  3.1 1.0 copy-start.2
  4.1 1.0 copy-start.3
  81.8 0.7 copy-start.4
  82.5 0.7 copy-start.5

commit v2 on v0

v2 whole, which is shorter than its diff:
```python
import functools

import jax
import jax.numpy as jnp
from jax import lax
from jax.experimental import pallas as pl
from jax.experimental.pallas import tpu as pltpu
from jax.sharding import PartitionSpec as P

HEAD = 128
BLOCK = 128
MAXT = 6
HEADS = 4
UNITS = 2 * HEADS
TILES = 24
PLUS = (1, 4, 6)
MESH = pl.DeviceIdType.MESH
LOG2E = 1.4426950408889634


def place():
    tm = lax.axis_index("tm")
    space = lax.axis_index("space")
    core = lax.rem(tm, 2)
    z_lo = lax.rem(lax.div(tm, 2), 4)
    x = lax.rem(space, 4)
    z_hi = lax.div(space, 4)
    return tm, core, x, z_hi, z_hi * 4 + z_lo


def ring_peers():
    tm, core, x, z_hi, z = place()

    def at(tm_step, z_step):
        there = lax.rem(z + z_step, 8)
        return {"tm": lax.rem(tm + tm_step, 32), "space": lax.div(there, 4) * 4 + x}

    right, left, far_right, far_left = at(2, 1), at(30, 7), at(2, 5), at(30, 3)
    partner = {"tm": tm + 1 - 2 * core, "space": z_hi * 4 + x}
    along_x = [{"tm": tm, "space": z_hi * 4 + lax.rem(x + d, 4)} for d in (1, 2, 3)]
    return right, left, far_right, far_left, partner, along_x


def meet(peers):
    barrier = pltpu.get_barrier_semaphore()
    for peer in peers:
        pl.semaphore_signal(barrier, inc=1, device_id=peer, device_id_type=MESH)
    pl.semaphore_wait(barrier, len(peers))


def send(src, dst, sems, index, device):
    send_sem, recv_sem = sems
    copy = pltpu.make_async_remote_copy(
        src_ref=src,
        dst_ref=dst,
        send_sem=send_sem.at[index],
        recv_sem=recv_sem.at[index],
        device_id=device,
        device_id_type=MESH,
    )
    copy.start()
    return copy


def columns(start, width):
    return pl.ds(pl.multiple_of(start, width), width)


NT = (((1,), (1,)), ((), ()))
NN = (((1,), (0,)), ((), ()))
TN = (((0,), (0,)), ((), ()))


def dot(a, b, dims):
    return lax.dot_general(a, b, dims, preferred_element_type=jnp.float32)


def add(*terms):
    out = terms[0].astype(jnp.float32)
    for term in terms[1:]:
        out = out + term.astype(jnp.float32)
    return out.astype(jnp.bfloat16)


def head_grads(h, half, tiles_ref, kinds_ref, kv_ref, q_ref, g_ref, slots, dq_ref):
    scale = 1.0 / HEAD**0.5
    row = lax.broadcasted_iota(jnp.int32, (BLOCK, 2 * BLOCK), 0)
    col = lax.broadcasted_iota(jnp.int32, (BLOCK, 2 * BLOCK), 1)
    ahead = row - jnp.where(col >= BLOCK, col - BLOCK, col)
    one, two = pl.ds(h * 256, HEAD), pl.ds(h * 256 + HEAD, HEAD)

    def block(b, carry):
        line = half * 4 + b
        names = [tiles_ref[line, m] for m in range(MAXT)]
        kinds = [kinds_ref[line, m] for m in range(MAXT)]
        k = jnp.concatenate([kv_ref[0, t] for t in names], axis=0)
        v = jnp.concatenate([kv_ref[1, t] for t in names], axis=0)
        q = jnp.concatenate([q_ref[b, :, one], q_ref[b, :, two]], axis=0)
        g = jnp.concatenate([g_ref[b, :, one], g_ref[b, :, two]], axis=0)
        scores = dot(k, q, NT)
        masked = []
        for m in range(MAXT):
            limit = jnp.where(kinds[m] == 0, BLOCK, jnp.where(kinds[m] == 1, 0, -2 * BLOCK))
            masked.append(
                jnp.where(ahead <= limit, scores[m * BLOCK : (m + 1) * BLOCK], -jnp.inf)
            )
        scores = jnp.concatenate(masked, axis=0)
        top = jnp.max(scores, axis=0, keepdims=True)
        weights = jnp.exp2((scores - top) * (scale * LOG2E))
        probs = weights * (1.0 / jnp.sum(weights, axis=0, keepdims=True))
        low = probs.astype(jnp.bfloat16)
        grad_probs = dot(v, g, NT)
        delta = jnp.sum(low.astype(jnp.float32) * grad_probs, axis=0, keepdims=True)
        grad_scores = (probs * (grad_probs - delta) * scale).astype(jnp.bfloat16)
        slots[1, b, :MAXT] = dot(low, g, NN).reshape(MAXT, BLOCK, HEAD)
        slots[0, b, :MAXT] = dot(grad_scores, q, NN).reshape(MAXT, BLOCK, HEAD)
        grad_q = dot(grad_scores, k, TN).astype(jnp.bfloat16)
        dq_ref[b, :, one] = grad_q[:BLOCK]
        dq_ref[b, :, two] = grad_q[BLOCK:]
        return carry

    lax.fori_loop(0, 4, block, 0)


def kernel(
    tiles_ref, kinds_ref, q_in, k_in, v_in, g_in, oq_ref, ok_ref, ov_ref,
    kv0, kv1, kv2, kv3, qh, gh, dq, slots, where, dkv,
    part, near, mid, back, summed, relay, total,
    xs, xr, qs, qr, s1, r1, s2, r2, s3, r3, sp, rp,
    os_, or_, ys, yr, t1, u1, t2, u2, t3, u3, tp, up, local, local_out,
):
    tm, core, x, z_hi, z = place()
    right, left, far_right, far_left, partner, along_x = ring_peers()
    from_left = lax.div(lax.rem(z + 7, 8), 4)
    from_far = 1 - from_left
    opposite = 1 - z_hi
    kv = (kv0, kv1, kv2, kv3)
    meet([right, left, far_right, far_left, partner] + along_x)

    def quad(window, half):
        return pl.ds(window * 8 + half * 4, 4)

    def buffer(unit):
        return kv[unit // 2].at[unit % 2]

    def source(unit, to_x):
        ref = v_in if unit % 2 else k_in
        return ref.at[:, columns((to_x * HEADS + unit // 2) * HEAD, HEAD)]

    def units(h):
        return (2 * h, 2 * h + 1)

    x_copies, own, q_copies = {}, {}, {}
    first, second, third, across = {}, {}, {}, {}
    out_q, out_x, own_out = [], [], []
    near_c, far_c, back_c, across_out = {}, {}, {}, {}

    def spread(h):
        for unit in units(h):
            there = buffer(unit).at[z_hi * 4 + x]
            x_copies[unit] = [
                send(source(unit, lax.rem(x + d, 4)), there, (xs, xr), unit * 3 + d - 1,
                     along_x[d - 1])
                for d in (1, 2, 3)
            ]
            own[unit] = pltpu.make_async_copy(source(unit, x), there, local.at[unit])
            own[unit].start()

    def spread_q(h):
        q_copies[h] = []
        for i, (ref, to) in enumerate(((q_in, qh), (g_in, gh))):
            there = to.at[x, :, pl.ds(h * 256, 256)]
            for d in (1, 2, 3):
                q_copies[h].append(
                    send(ref.at[:, columns(lax.rem(x + d, 4) * 1024 + h * 256, 256)], there,
                         (qs, qr), h * 6 + i * 3 + d - 1, along_x[d - 1])
                )
            mine = pltpu.make_async_copy(
                ref.at[:, columns(x * 1024 + h * 256, 256)], there,
                local.at[UNITS + 2 * h + i])
            mine.start()
            own[UNITS + 2 * h + i] = mine

    def start(h):
        for unit in units(h):
            own[unit].wait()
            for copy in x_copies[unit]:
                copy.wait_recv()
            piece = buffer(unit).at[quad(0, z_hi)]
            there = buffer(unit).at[quad(2, z_hi)]
            if unit not in PLUS:
                second[unit] = send(piece, there, (s2, r2), unit, far_right)
            first[unit] = send(piece, there, (s1, r1), unit, right)

    def hop(h):
        for unit in units(h):
            buf = buffer(unit)
            if unit in PLUS:
                first[unit].wait_recv()
                second[unit] = send(buf.at[quad(2, from_left)], buf.at[quad(0, from_left)],
                                    (s2, r2), unit, far_left)
            else:
                second[unit].wait_recv()
                third[unit] = send(buf.at[quad(2, from_far)], buf.at[quad(0, from_far)],
                                   (s3, r3), unit, left)

    def last_hop(h):
        for unit in units(h):
            if unit in PLUS:
                buf = buffer(unit)
                second[unit].wait_recv()
                third[unit] = send(buf.at[quad(0, opposite)], buf.at[quad(2, opposite)],
                                   (s3, r3), unit, right)

    def share(h):
        for unit in units(h):
            buf = buffer(unit)
            if unit not in PLUS:
                first[unit].wait_recv()
            third[unit].wait_recv()
            across[unit] = send(buf.at[pl.ds(core * 16, 8)], buf.at[pl.ds(8, 8)],
                                (sp, rp), unit, partner)

    def compute(h):
        for unit in units(h):
            across[unit].wait_recv()
        for copy in q_copies[h]:
            copy.wait_recv()
        own[UNITS + 2 * h].wait()
        own[UNITS + 2 * h + 1].wait()
        head_grads(h, z_hi, tiles_ref, kinds_ref, kv[h], qh, gh, slots, dq)

        def tile(t, carry):
            for i in (0, 1):
                terms = [slots[i, b, where[b * TILES + t]] for b in range(4)]
                dkv[2 * h + i, t] = ((terms[0] + terms[1]) + (terms[2] + terms[3])).astype(
                    jnp.bfloat16
                )
            return carry

        lax.fori_loop(0, TILES, tile, 0)
        for unit in units(h):
            across_out[unit] = send(dkv.at[unit, pl.ds(8, 8)], part.at[unit], (tp, up), unit,
                                    partner)
        there = oq_ref.at[:, columns(x * 1024 + h * 256, 256)]
        for d in (1, 2, 3):
            out_q.append(
                send(dq.at[lax.rem(x + d, 4), :, pl.ds(h * 256, 256)], there, (os_, or_),
                     h * 3 + d - 1, along_x[d - 1])
            )
        mine = pltpu.make_async_copy(dq.at[x, :, pl.ds(h * 256, 256)], there,
                                     local_out.at[UNITS + h])
        mine.start()
        own_out.append(mine)

    def fold(h):
        for unit in units(h):
            across_out[unit].wait_recv()
            summed[unit, pl.ds(core * 8, 8)] = add(dkv[unit, pl.ds(core * 16, 8)], part[unit])
            summed[unit, pl.ds(8 - core * 8, 8)] = dkv[unit, pl.ds(16 - core * 16, 8)]
            if unit in PLUS:
                near_c[unit] = send(summed.at[unit, quad(1, from_far)], near.at[unit],
                                    (t1, u1), unit, left)
            else:
                near_c[unit] = send(summed.at[unit, quad(0, opposite)], near.at[unit],
                                    (t1, u1), unit, right)

    def pass_on(h):
        for unit in units(h):
            near_c[unit].wait_recv()
            if unit in PLUS:
                relay[unit] = add(near[unit], summed[unit, quad(0, opposite)])
                far_c[unit] = send(relay.at[unit], mid.at[unit], (t2, u2), unit, far_right)
            else:
                relay[unit] = add(near[unit], summed[unit, quad(1, from_far)])
                far_c[unit] = send(relay.at[unit], mid.at[unit], (t2, u2), unit, far_left)
                back_c[unit] = send(summed.at[unit, quad(1, from_left)], back.at[unit],
                                    (t3, u3), unit, left)

    def turn(h):
        for unit in units(h):
            if unit in PLUS:
                far_c[unit].wait_recv()
                total[unit] = add(mid[unit], summed[unit, quad(1, from_left)])
                back_c[unit] = send(total.at[unit], back.at[unit], (t3, u3), unit, left)

    def finish(h):
        for unit in units(h):
            back_c[unit].wait_recv()
            if unit in PLUS:
                back_c[unit].wait_send()
                total[unit] = add(summed[unit, quad(0, z_hi)], back[unit])
            else:
                far_c[unit].wait_recv()
                total[unit] = add(summed[unit, quad(0, z_hi)], mid[unit], back[unit])
            ref = ov_ref if unit % 2 else ok_ref
            there = ref.at[:, columns((x * HEADS + unit // 2) * HEAD, HEAD)]
            for d in (1, 2, 3):
                out_x.append(
                    send(total.at[unit, lax.rem(x + d, 4)], there, (ys, yr), unit * 3 + d - 1,
                         along_x[d - 1])
                )
            mine = pltpu.make_async_copy(total.at[unit, x], there, local_out.at[unit])
            mine.start()
            own_out.append(mine)

    def find_slots():
        def one(t, carry):
            for b in range(4):
                found = MAXT
                for m in reversed(range(MAXT)):
                    found = jnp.where(tiles_ref[z_hi * 4 + b, m] == t, m, found)
                where[b * TILES + t] = found
            return carry

        lax.fori_loop(0, TILES, one, 0)
        for i in (0, 1):
            for b in range(4):
                slots[i, b, MAXT] = jnp.zeros((BLOCK, HEAD), jnp.float32)

    for step, h in ((spread, 0), (spread, 1), (spread_q, 0), (spread, 2), (spread_q, 1),
                    (spread, 3), (spread_q, 2), (spread_q, 3)):
        step(h)
    start(0)
    start(1)
    find_slots()
    for step, h in ORDER:
        {"start": start, "hop": hop, "last_hop": last_hop, "share": share, "compute": compute,
         "fold": fold, "pass_on": pass_on, "turn": turn, "finish": finish}[step](h)

    for copy in out_q + out_x:
        copy.wait_recv()
    for mine in own_out:
        mine.wait()
    sent = [c for table in (x_copies, q_copies) for copies in table.values() for c in copies]
    for table in (first, second, third, across, near_c, far_c, across_out):
        sent += list(table.values())
    sent += [back_c[unit] for unit in range(UNITS) if unit not in PLUS] + out_q + out_x
    for copy in sent:
        copy.wait_send()


ORDER = (
    ("hop", 0), ("start", 2), ("last_hop", 0), ("hop", 1), ("share", 0),
    ("compute", 0),
    ("start", 3), ("last_hop", 1), ("hop", 2), ("share", 1), ("fold", 0),
    ("compute", 1),
    ("pass_on", 0), ("last_hop", 2), ("hop", 3), ("share", 2), ("fold", 1),
    ("compute", 2),
    ("turn", 0), ("pass_on", 1), ("last_hop", 3), ("share", 3), ("fold", 2),
    ("compute", 3),
    ("finish", 0), ("turn", 1), ("pass_on", 2), ("fold", 3),
    ("finish", 1), ("turn", 2), ("pass_on", 3),
    ("finish", 2), ("turn", 3), ("finish", 3),
)


def body(queries, keys, values, output_gradient, tiles, kinds):
    vmem = pl.BlockSpec(memory_space=pltpu.VMEM)
    smem = pl.BlockSpec(memory_space=pltpu.SMEM)
    anywhere = pl.BlockSpec(memory_space=pl.ANY)
    dma = pltpu.SemaphoreType.DMA
    bf16 = jnp.bfloat16
    unit = pltpu.VMEM((UNITS, 4, BLOCK, HEAD), bf16)
    rows = pltpu.VMEM((4, BLOCK, 1024), bf16)
    return pl.pallas_call(
        kernel,
        name="attention_grads",
        out_shape=(
            jax.ShapeDtypeStruct((BLOCK, 4096), bf16),
            jax.ShapeDtypeStruct((BLOCK, 2048), bf16),
            jax.ShapeDtypeStruct((BLOCK, 2048), bf16),
        ),
        in_specs=[smem, smem] + [anywhere] * 4,
        out_specs=(vmem,) * 3,
        scratch_shapes=[pltpu.VMEM((2, TILES, BLOCK, HEAD), bf16)] * HEADS
        + [rows] * 3
        + [
            pltpu.VMEM((2, 4, MAXT + 1, BLOCK, HEAD), jnp.float32),
            pltpu.SMEM((4 * TILES,), jnp.int32),
            pltpu.VMEM((UNITS, TILES, BLOCK, HEAD), bf16),
            pltpu.VMEM((UNITS, 8, BLOCK, HEAD), bf16),
            unit,
            unit,
            unit,
            pltpu.VMEM((UNITS, 16, BLOCK, HEAD), bf16),
            unit,
            unit,
        ]
        + [dma((24,))] * 4
        + [dma((UNITS,))] * 8
        + [dma((12,))] * 2
        + [dma((24,))] * 2
        + [dma((UNITS,))] * 8
        + [dma((2 * UNITS,)), dma((UNITS + HEADS,))],
        compiler_params=pltpu.CompilerParams(
            collective_id=1, has_side_effects=True, vmem_limit_bytes=60 << 20
        ),
    )(tiles, kinds, queries, keys, values, output_gradient)


def solution(mesh):
    rows = P(("tm", "space"), None)
    return jax.shard_map(
        body,
        mesh=mesh,
        in_specs=(rows, rows, rows, rows, P("tm", None), P("tm", None)),
        out_specs=(rows, rows, rows),
        check_vma=False,
    )
```

time: 463 us -> 178 us (0.38); the launches traced: 454 us -> 178 us
  Pallas kernels: 0 us -> 173 us
  waiting for transfers between devices: 138 us -> 0 us
  local copies, waits for them, and re-layouts: 125 us -> 4.37 us
  starting transfers between devices: 87.7 us -> 0 us
  other arithmetic: 61.8 us -> 0 us
  matrix products: 39.5 us -> 0 us
    pallas_call x0 -> x1, Pallas kernels: none -> 173 us  [body(): pl.pallas_call(kernel, name='attention_grads', out_shape=(jax.ShapeDtypeS...]
    ppermute x8 -> x0, waiting for transfers between devices: 99.9 us -> none  [shifted_2(): return lax.ppermute(block, axis, route)]
    all_to_all x7 -> x0, starting transfers between devices: 61.7 us -> none  [the longest x1 11.5 us: body(): lax.all_to_all(keys, 'space', split_axis=1, concat_axis=0, tiled=True)]
    dot_general x12 -> x0, matrix products: 39.5 us -> none  [the longest x2 8.65 us: block_grads(): jnp.einsum('qkgd,tkd->kgqt', grad_rows, value_flat, preferred_element_typ...]
    all_to_all x7 -> x0, waiting for transfers between devices: 38.3 us -> none  [the longest x1 12.2 us: body(): lax.all_to_all(queries, 'space', split_axis=1, concat_axis=0, tiled=True)]
    scatter-add x4 -> x0, other arithmetic: 37.7 us -> none  [the longest x2 19.2 us: one_round(): summed_value_grad.at[flat_tiles]]
    gather x4 -> x0, local copies, waits for them, and re-layouts: 28.3 us -> none  [the longest x2 14.8 us: one_round(): value_tiles[tile_part]]
    reshape x12 -> x0, local copies, waits for them, and re-layouts: 27.6 us -> none  [the longest x2 9.91 us: block_grads(): value_flat = value_tiles.reshape(blocks * length, kv_count, head_dim)]
  transfers between devices with their start and end apart: 15 -> 0, of which waited for: 9 -> 0; matrix products, arithmetic and copies ran while one was open for 7% -> 0% of each run, Pallas kernels for 0% -> 0%
where the time goes in v2:
time: 178 us
  Pallas kernels  173 us (97%)
  local copies, waits for them, and re-layouts  4.37 us (2%)
    pallas_call x1, Pallas kernels, body(): pl.pallas_call(kernel, name='attention_grads', out_shape=(jax.ShapeDtypeS...  173 us
    unnamed x7, local copies, waits for them, and re-layouts  4.37 us

profile of v2, /device:TPU:2, one launch (start us, length us, event | category | flops | bytes accessed | tf_op | source)
XLA Modules:
  0.0 177.8 jit_solution(13941156424153398595)
XLA Ops:
  0.6 172.8 %attention_grads.1 = (bf16[128,4096]{1,0:T(8,128)(2,1)}, bf16[128,2048]{1,0:T(8,128)(2,1)}, bf16[128,2048]{1,0:T(8,128)(2,1)}) custom-call(s32[8,6]{1,0:T(8,128)} %tiles_ref.1, s32[8,6]{1,0:T(8,128)} %kinds_ref.1, bf16[128,4096]{1,0:T(8,128)(2,1)} %q_in.1, bf16[128,2048]{1,0:T(8,128)(2,1)} %k_in.1, bf16[128,2048]{1,0:T(8,128)(2,1)} %v_in.1, ...), custom_call_target="tpu_custom_call" | custom-call | tf_op jit(solution)/shard_map/attention_grads/pallas_call | solution.py:366
  173.4 0.0 copy-start.1
  173.4 2.3 %copy.12 = bf16[128,4096]{1,0:T(8,128)(2,1)} copy(bf16[128,4096]{1,0:T(8,128)(2,1)} %get-tuple-element.6) | data formatting | bytes 2097152
  175.8 0.0 copy-done.1
  175.8 0.0 copy-start
  175.8 0.8 copy.13
  176.6 0.4 copy-done
  177.0 0.8 copy.14
Async XLA Ops:
  173.4 2.4 %copy-start.1 = (bf16[128,2048]{1,0:T(8,128)(2,1)S(1)}, bf16[128,2048]{1,0:T(8,128)(2,1)}, u32[]{:S(2)}) copy-start(bf16[128,2048]{1,0:T(8,128)(2,1)} %get-tuple-element.7) | copy-start | bytes 1572868
  175.8 1.2 copy-start

commit v3 on v2

--- a/solution.py
+++ b/solution.py
@@ -14,6 +14,7 @@
 UNITS = 2 * HEADS
 TILES = 24
 PLUS = (1, 4, 6)
+OUT_PLUS = (1, 4, 6)
 MESH = pl.DeviceIdType.MESH
 LOG2E = 1.4426950408889634
 
@@ -147,16 +148,13 @@
         ref = v_in if unit % 2 else k_in
         return ref.at[:, columns((to_x * HEADS + unit // 2) * HEAD, HEAD)]
 
-    def units(h):
-        return (2 * h, 2 * h + 1)
-
     x_copies, own, q_copies = {}, {}, {}
     first, second, third, across = {}, {}, {}, {}
     out_q, out_x, own_out = [], [], []
     near_c, far_c, back_c, across_out = {}, {}, {}, {}
 
     def spread(h):
-        for unit in units(h):
+        for unit in (2 * h, 2 * h + 1):
             there = buffer(unit).at[z_hi * 4 + x]
             x_copies[unit] = [
                 send(source(unit, lax.rem(x + d, 4)), there, (xs, xr), unit * 3 + d - 1,
@@ -181,48 +179,53 @@
             mine.start()
             own[UNITS + 2 * h + i] = mine
 
-    def start(h):
-        for unit in units(h):
+    def arrive(unit):
+        if unit not in arrived:
             own[unit].wait()
             for copy in x_copies[unit]:
                 copy.wait_recv()
-            piece = buffer(unit).at[quad(0, z_hi)]
-            there = buffer(unit).at[quad(2, z_hi)]
-            if unit not in PLUS:
-                second[unit] = send(piece, there, (s2, r2), unit, far_right)
-            first[unit] = send(piece, there, (s1, r1), unit, right)
-
-    def hop(h):
-        for unit in units(h):
-            buf = buffer(unit)
-            if unit in PLUS:
-                first[unit].wait_recv()
-                second[unit] = send(buf.at[quad(2, from_left)], buf.at[quad(0, from_left)],
-                                    (s2, r2), unit, far_left)
-            else:
-                second[unit].wait_recv()
-                third[unit] = send(buf.at[quad(2, from_far)], buf.at[quad(0, from_far)],
-                                   (s3, r3), unit, left)
-
-    def last_hop(h):
-        for unit in units(h):
-            if unit in PLUS:
-                buf = buffer(unit)
-                second[unit].wait_recv()
-                third[unit] = send(buf.at[quad(0, opposite)], buf.at[quad(2, opposite)],
-                                   (s3, r3), unit, right)
-
-    def share(h):
-        for unit in units(h):
-            buf = buffer(unit)
-            if unit not in PLUS:
-                first[unit].wait_recv()
-            third[unit].wait_recv()
-            across[unit] = send(buf.at[pl.ds(core * 16, 8)], buf.at[pl.ds(8, 8)],
-                                (sp, rp), unit, partner)
+            arrived.add(unit)
+
+    def begin(unit):
+        arrive(unit)
+        if unit in PLUS:
+            to_right(unit)
+        else:
+            second[unit] = send(buffer(unit).at[quad(0, z_hi)], buffer(unit).at[quad(2, z_hi)],
+                                (s2, r2), unit, far_right)
+
+    def to_right(unit):
+        arrive(unit)
+        first[unit] = send(buffer(unit).at[quad(0, z_hi)], buffer(unit).at[quad(2, z_hi)],
+                           (s1, r1), unit, right)
+
+    def hop(unit):
+        buf = buffer(unit)
+        if unit in PLUS:
+            first[unit].wait_recv()
+            second[unit] = send(buf.at[quad(2, from_left)], buf.at[quad(0, from_left)],
+                                (s2, r2), unit, far_left)
+        else:
+            second[unit].wait_recv()
+            third[unit] = send(buf.at[quad(2, from_far)], buf.at[quad(0, from_far)],
+                               (s3, r3), unit, left)
+
+    def last_hop(unit):
+        buf = buffer(unit)
+        second[unit].wait_recv()
+        third[unit] = send(buf.at[quad(0, opposite)], buf.at[quad(2, opposite)],
+                           (s3, r3), unit, right)
+
+    def share(unit):
+        buf = buffer(unit)
+        if unit not in PLUS:
+            first[unit].wait_recv()
+        third[unit].wait_recv()
+        across[unit] = send(buf.at[pl.ds(core * 16, 8)], buf.at[pl.ds(8, 8)],
+                            (sp, rp), unit, partner)
 
     def compute(h):
-        for unit in units(h):
+        for unit in (2 * h, 2 * h + 1):
             across[unit].wait_recv()
         for copy in q_copies[h]:
             copy.wait_recv()
@@ -239,7 +242,7 @@
             return carry
 
         lax.fori_loop(0, TILES, tile, 0)
-        for unit in units(h):
+        for unit in (2 * h, 2 * h + 1):
             across_out[unit] = send(dkv.at[unit, pl.ds(8, 8)], part.at[unit], (tp, up), unit,
                                     partner)
         there = oq_ref.at[:, columns(x * 1024 + h * 256, 256)]
@@ -253,58 +256,55 @@
         mine.start()
         own_out.append(mine)
 
-    def fold(h):
-        for unit in units(h):
-            across_out[unit].wait_recv()
-            summed[unit, pl.ds(core * 8, 8)] = add(dkv[unit, pl.ds(core * 16, 8)], part[unit])
-            summed[unit, pl.ds(8 - core * 8, 8)] = dkv[unit, pl.ds(16 - core * 16, 8)]
-            if unit in PLUS:
-                near_c[unit] = send(summed.at[unit, quad(1, from_far)], near.at[unit],
-                                    (t1, u1), unit, left)
-            else:
-                near_c[unit] = send(summed.at[unit, quad(0, opposite)], near.at[unit],
-                                    (t1, u1), unit, right)
-
-    def pass_on(h):
-        for unit in units(h):
-            near_c[unit].wait_recv()
-            if unit in PLUS:
-                relay[unit] = add(near[unit], summed[unit, quad(0, opposite)])
-                far_c[unit] = send(relay.at[unit], mid.at[unit], (t2, u2), unit, far_right)
-            else:
-                relay[unit] = add(near[unit], summed[unit, quad(1, from_far)])
-                far_c[unit] = send(relay.at[unit], mid.at[unit], (t2, u2), unit, far_left)
-                back_c[unit] = send(summed.at[unit, quad(1, from_left)], back.at[unit],
-                                    (t3, u3), unit, left)
-
-    def turn(h):
-        for unit in units(h):
-            if unit in PLUS:
-                far_c[unit].wait_recv()
-                total[unit] = add(mid[unit], summed[unit, quad(1, from_left)])
-                back_c[unit] = send(total.at[unit], back.at[unit], (t3, u3), unit, left)
-
-    def finish(h):
-        for unit in units(h):
-            back_c[unit].wait_recv()
-            if unit in PLUS:
-                back_c[unit].wait_send()
-                total[unit] = add(summed[unit, quad(0, z_hi)], back[unit])
-            else:
-                far_c[unit].wait_recv()
-                total[unit] = add(summed[unit, quad(0, z_hi)], mid[unit], back[unit])
-            ref = ov_ref if unit % 2 else ok_ref
-            there = ref.at[:, columns((x * HEADS + unit // 2) * HEAD, HEAD)]
-            for d in (1, 2, 3):
-                out_x.append(
-                    send(total.at[unit, lax.rem(x + d, 4)], there, (ys, yr), unit * 3 + d - 1,
-                         along_x[d - 1])
-                )
-            mine = pltpu.make_async_copy(total.at[unit, x], there, local_out.at[unit])
-            mine.start()
-            own_out.append(mine)
-
-    def find_slots():
+    def fold(unit):
+        across_out[unit].wait_recv()
+        summed[unit, pl.ds(core * 8, 8)] = add(dkv[unit, pl.ds(core * 16, 8)], part[unit])
+        summed[unit, pl.ds(8 - core * 8, 8)] = dkv[unit, pl.ds(16 - core * 16, 8)]
+        if unit in OUT_PLUS:
+            near_c[unit] = send(summed.at[unit, quad(1, from_far)], near.at[unit],
+                                (t1, u1), unit, left)
+        else:
+            near_c[unit] = send(summed.at[unit, quad(0, opposite)], near.at[unit],
+                                (t1, u1), unit, right)
+
+    def give_back(unit):
+        back_c[unit] = send(summed.at[unit, quad(1, from_left)], back.at[unit],
+                            (t3, u3), unit, left)
+
+    def pass_on(unit):
+        near_c[unit].wait_recv()
+        if unit in OUT_PLUS:
+            relay[unit] = add(near[unit], summed[unit, quad(0, opposite)])
+            far_c[unit] = send(relay.at[unit], mid.at[unit], (t2, u2), unit, far_right)
+        else:
+            relay[unit] = add(near[unit], summed[unit, quad(1, from_far)])
+            far_c[unit] = send(relay.at[unit], mid.at[unit], (t2, u2), unit, far_left)
+
+    def turn(unit):
+        far_c[unit].wait_recv()
+        total[unit] = add(mid[unit], summed[unit, quad(1, from_left)])
+        back_c[unit] = send(total.at[unit], back.at[unit], (t3, u3), unit, left)
+
+    def finish(unit):
+        back_c[unit].wait_recv()
+        if unit in OUT_PLUS:
+            back_c[unit].wait_send()
+            total[unit] = add(summed[unit, quad(0, z_hi)], back[unit])
+        else:
+            far_c[unit].wait_recv()
+            total[unit] = add(summed[unit, quad(0, z_hi)], mid[unit], back[unit])
+        ref = ov_ref if unit % 2 else ok_ref
+        there = ref.at[:, columns((x * HEADS + unit // 2) * HEAD, HEAD)]
+        for d in (1, 2, 3):
+            out_x.append(
+                send(total.at[unit, lax.rem(x + d, 4)], there, (ys, yr), unit * 3 + d - 1,
+                     along_x[d - 1])
+            )
+        mine = pltpu.make_async_copy(total.at[unit, x], there, local_out.at[unit])
+        mine.start()
+        own_out.append(mine)
+
+    def find_slots(_):
         def one(t, carry):
             for b in range(4):
                 found = MAXT
@@ -318,15 +318,12 @@
             for b in range(4):
                 slots[i, b, MAXT] = jnp.zeros((BLOCK, HEAD), jnp.float32)
 
-    for step, h in ((spread, 0), (spread, 1), (spread_q, 0), (spread, 2), (spread_q, 1),
-                    (spread, 3), (spread_q, 2), (spread_q, 3)):
-        step(h)
-    start(0)
-    start(1)
-    find_slots()
-    for step, h in ORDER:
-        {"start": start, "hop": hop, "last_hop": last_hop, "share": share, "compute": compute,
-         "fold": fold, "pass_on": pass_on, "turn": turn, "finish": finish}[step](h)
+    arrived = set()
+    steps = {"X": spread, "Q": spread_q, "a": begin, "b": to_right, "c": hop, "d": share,
+             "e": last_hop, "K": compute, "f": fold, "g": give_back, "p": pass_on, "t": turn,
+             "y": finish, "w": find_slots}
+    for name in ORDER:
+        steps[name[0]](int(name[1]))
 
     for copy in out_q + out_x:
         copy.wait_recv()
@@ -335,23 +332,19 @@
     sent = [c for table in (x_copies, q_copies) for copies in table.values() for c in copies]
     for table in (first, second, third, across, near_c, far_c, across_out):
         sent += list(table.values())
-    sent += [back_c[unit] for unit in range(UNITS) if unit not in PLUS] + out_q + out_x
+    sent += [back_c[unit] for unit in range(UNITS) if unit not in OUT_PLUS] + out_q + out_x
     for copy in sent:
         copy.wait_send()
 
 
 ORDER = (
-    ("hop", 0), ("start", 2), ("last_hop", 0), ("hop", 1), ("share", 0),
-    ("compute", 0),
-    ("start", 3), ("last_hop", 1), ("hop", 2), ("share", 1), ("fold", 0),
-    ("compute", 1),
-    ("pass_on", 0), ("last_hop", 2), ("hop", 3), ("share", 2), ("fold", 1),
-    ("compute", 2),
-    ("turn", 0), ("pass_on", 1), ("last_hop", 3), ("share", 3), ("fold", 2),
-    ("compute", 3),
-    ("finish", 0), ("turn", 1), ("pass_on", 2), ("fold", 3),
-    ("finish", 1), ("turn", 2), ("pass_on", 3),
-    ("finish", 2), ("turn", 3), ("finish", 3),
+    "X0", "X1", "X2", "X3", "b0", "a0", "a1", "w0", "b2", "a2", "b3", "a4",
+    "Q0", "c1", "a3", "Q1", "c0", "a6", "c4", "Q2", "c2", "Q3", "a5", "e1",
+    "c6", "c3", "d0", "d2", "a7", "e4", "d1", "K0", "d3", "b5", "c5", "b7",
+    "f0", "g0", "e6", "f1", "d4", "K1", "c7", "d5", "f2", "g2", "p0", "f3",
+    "g3", "K2", "p1", "p2", "d6", "d7", "f4", "f5", "K3", "y0", "p3", "g5",
+    "f6", "f7", "g7", "t1", "p4", "y2", "p5", "p6", "y1", "y3", "p7", "t4",
+    "y5", "t6", "y4", "y6", "y7",
 )
 
 

time: 178 us -> 158 us (0.89); the launches traced: 178 us -> 156 us
  Pallas kernels: 173 us -> 151 us
    pallas_call x1, Pallas kernels: 173 us -> 151 us  [body(): pl.pallas_call(kernel, name='attention_grads', out_shape=(jax.ShapeDtypeS...]
where the time goes in v3:
time: 158 us; the launch traced here: 156 us
  Pallas kernels  151 us (96%)
  local copies, waits for them, and re-layouts  4.37 us (3%)
    pallas_call x1, Pallas kernels, body(): pl.pallas_call(kernel, name='attention_grads', out_shape=(jax.ShapeDtypeS...  151 us
    unnamed x7, local copies, waits for them, and re-layouts  4.37 us

profile of v3, /device:TPU:2, one launch (start us, length us, event | category | flops | bytes accessed | tf_op | source)
XLA Modules:
  0.0 155.5 jit_solution(9764960138228192358)
XLA Ops:
  0.6 150.5 %attention_grads.1 = (bf16[128,4096]{1,0:T(8,128)(2,1)}, bf16[128,2048]{1,0:T(8,128)(2,1)}, bf16[128,2048]{1,0:T(8,128)(2,1)}) custom-call(s32[8,6]{1,0:T(8,128)} %tiles_ref.1, s32[8,6]{1,0:T(8,128)} %kinds_ref.1, bf16[128,4096]{1,0:T(8,128)(2,1)} %q_in.1, bf16[128,2048]{1,0:T(8,128)(2,1)} %k_in.1, bf16[128,2048]{1,0:T(8,128)(2,1)} %v_in.1, ...), custom_call_target="tpu_custom_call" | custom-call | tf_op jit(solution)/shard_map/attention_grads/pallas_call | solution.py:359
  151.2 0.0 copy-start.1
  151.2 2.3 %copy.12 = bf16[128,4096]{1,0:T(8,128)(2,1)} copy(bf16[128,4096]{1,0:T(8,128)(2,1)} %get-tuple-element.6) | data formatting | bytes 2097152
  153.5 0.0 copy-done.1
  153.5 0.0 copy-start
  153.5 0.8 copy.13
  154.3 0.4 copy-done
  154.8 0.8 copy.14
Async XLA Ops:
  151.2 2.4 %copy-start.1 = (bf16[128,2048]{1,0:T(8,128)(2,1)S(1)}, bf16[128,2048]{1,0:T(8,128)(2,1)}, u32[]{:S(2)}) copy-start(bf16[128,2048]{1,0:T(8,128)(2,1)} %get-tuple-element.7) | copy-start | bytes 1572868
  153.5 1.2 copy-start

commit v4 on v3

--- a/solution.py
+++ b/solution.py
@@ -15,6 +15,7 @@
 TILES = 24
 PLUS = (1, 4, 6)
 OUT_PLUS = (1, 4, 6)
+EARLY = (0, 1)
 MESH = pl.DeviceIdType.MESH
 LOG2E = 1.4426950408889634
 
@@ -61,6 +62,19 @@
     )
     copy.start()
     return copy
+
+
+class Pieces:
+    def __init__(self):
+        self.copies = []
+
+    def wait_recv(self):
+        for copy in self.copies:
+            copy.wait_recv()
+
+    def wait_send(self):
+        for copy in self.copies:
+            copy.wait_send()
 
 
 def columns(start, width):
@@ -128,7 +142,7 @@
     kv0, kv1, kv2, kv3, qh, gh, dq, slots, where, dkv,
     part, near, mid, back, summed, relay, total,
     xs, xr, qs, qr, s1, r1, s2, r2, s3, r3, sp, rp,
-    os_, or_, ys, yr, t1, u1, t2, u2, t3, u3, tp, up, local, local_out,
+    os_, or_, ys, yr, t1, u1, t2, u2, t3, u3, tp, up, e1s, e1r, e2s, e2r, local, local_out,
 ):
     tm, core, x, z_hi, z = place()
     right, left, far_right, far_left, partner, along_x = ring_peers()
@@ -199,6 +213,26 @@
         first[unit] = send(buffer(unit).at[quad(0, z_hi)], buffer(unit).at[quad(2, z_hi)],
                            (s1, r1), unit, right)
 
+    for unit in EARLY:
+        first[unit] = Pieces()
+        if unit not in PLUS:
+            second[unit] = Pieces()
+
+    def block_on(unit, step):
+        at = z_hi * 4 + lax.rem(x + 4 - step, 4)
+        if step:
+            x_copies[unit][step - 1].wait_recv()
+            piece = buffer(unit).at[at]
+        else:
+            piece = source(unit, x)
+        there = buffer(unit).at[16 + at]
+        if unit not in PLUS:
+            second[unit].copies.append(
+                send(piece, there, (e2s, e2r), unit * 4 + step, far_right))
+        first[unit].copies.append(send(piece, there, (e1s, e1r), unit * 4 + step, right))
+        if step == 2:
+            own[unit].wait()
+
     def hop(unit):
         buf = buffer(unit)
         if unit in PLUS:
@@ -321,7 +355,9 @@
     arrived = set()
     steps = {"X": spread, "Q": spread_q, "a": begin, "b": to_right, "c": hop, "d": share,
              "e": last_hop, "K": compute, "f": fold, "g": give_back, "p": pass_on, "t": turn,
-             "y": finish, "w": find_slots}
+             "y": finish, "w": find_slots,
+             "i": lambda u: block_on(u, 0), "j": lambda u: block_on(u, 1),
+             "k": lambda u: block_on(u, 3), "l": lambda u: block_on(u, 2)}
     for name in ORDER:
         steps[name[0]](int(name[1]))
 
@@ -338,25 +374,58 @@
 
 
 ORDER = (
-    "X0", "X1", "X2", "X3", "b0", "a0", "a1", "w0", "b2", "a2", "b3", "a4",
-    "Q0", "c1", "a3", "Q1", "c0", "a6", "c4", "Q2", "c2", "Q3", "a5", "e1",
-    "c6", "c3", "d0", "d2", "a7", "e4", "d1", "K0", "d3", "b5", "c5", "b7",
-    "f0", "g0", "e6", "f1", "d4", "K1", "c7", "d5", "f2", "g2", "p0", "f3",
-    "g3", "K2", "p1", "p2", "d6", "d7", "f4", "f5", "K3", "y0", "p3", "g5",
-    "f6", "f7", "g7", "t1", "p4", "y2", "p5", "p6", "y1", "y3", "p7", "t4",
-    "y5", "t6", "y4", "y6", "y7",
+    "X0", "i0", "i1", "X1", "j0", "k0", "X2", "j1", "k1", "l0", "X3", "l1",
+    "w0", "b2", "a2", "Q0", "b3", "a3", "c1", "Q1", "a4", "c0", "a6", "Q2",
+    "a5", "c2", "b5", "Q3", "e1", "c4", "c6", "c3", "d0", "a7", "d1", "K0",
+    "c5", "d2", "f0", "d3", "f1", "e4", "K1", "g0", "b7", "e6", "f2", "p0",
+    "g2", "f3", "g3", "d5", "c7", "p1", "d4", "K2", "d6", "p2", "f4", "f5",
+    "d7", "g5", "K3", "y0", "p3", "f6", "f7", "g7", "p4", "p6", "y2", "p5",
+    "t1", "y3", "p7", "t4", "t6", "y1", "y5", "y4", "y6", "y7",
 )
 
 
+def copy_kernel(*refs):
+    ins, outs, bufs, into, out_of = refs[:3], refs[3:6], refs[6:9], refs[9], refs[10]
+    pieces = []
+    for i in range(3):
+        for part in range(4):
+            rows = pl.ds(part * 32, 32)
+            n = i * 4 + part
+            pieces.append((
+                pltpu.make_async_copy(ins[i].at[rows], bufs[i].at[rows], into.at[n]),
+                pltpu.make_async_copy(bufs[i].at[rows], outs[i].at[rows], out_of.at[n]),
+            ))
+    for load, _ in pieces:
+        load.start()
+    for load, store in pieces:
+        load.wait()
+        store.start()
+    for _, store in pieces:
+        store.wait()
+
+
+def copy_out(*arrays):
+    anywhere = pl.BlockSpec(memory_space=pl.ANY)
+    return pl.pallas_call(
+        copy_kernel,
+        name="copy_out",
+        out_shape=tuple(jax.ShapeDtypeStruct(a.shape, a.dtype) for a in arrays),
+        in_specs=[anywhere] * 3,
+        out_specs=(anywhere,) * 3,
+        scratch_shapes=[pltpu.VMEM(a.shape, a.dtype) for a in arrays]
+        + [pltpu.SemaphoreType.DMA((12,))] * 2,
+        compiler_params=pltpu.CompilerParams(vmem_limit_bytes=60 << 20),
+    )(*arrays)
+
+
 def body(queries, keys, values, output_gradient, tiles, kinds):
-    vmem = pl.BlockSpec(memory_space=pltpu.VMEM)
     smem = pl.BlockSpec(memory_space=pltpu.SMEM)
     anywhere = pl.BlockSpec(memory_space=pl.ANY)
     dma = pltpu.SemaphoreType.DMA
     bf16 = jnp.bfloat16
     unit = pltpu.VMEM((UNITS, 4, BLOCK, HEAD), bf16)
     rows = pltpu.VMEM((4, BLOCK, 1024), bf16)
-    return pl.pallas_call(
+    return copy_out(*pl.pallas_call(
         kernel,
         name="attention_grads",
         out_shape=(
@@ -365,7 +434,7 @@
             jax.ShapeDtypeStruct((BLOCK, 2048), bf16),
         ),
         in_specs=[smem, smem] + [anywhere] * 4,
-        out_specs=(vmem,) * 3,
+        out_specs=(anywhere,) * 3,
         scratch_shapes=[pltpu.VMEM((2, TILES, BLOCK, HEAD), bf16)] * HEADS
         + [rows] * 3
         + [
@@ -385,11 +454,12 @@
         + [dma((12,))] * 2
         + [dma((24,))] * 2
         + [dma((UNITS,))] * 8
+        + [dma((4 * len(EARLY),))] * 4
         + [dma((2 * UNITS,)), dma((UNITS + HEADS,))],
         compiler_params=pltpu.CompilerParams(
             collective_id=1, has_side_effects=True, vmem_limit_bytes=60 << 20
         ),
-    )(tiles, kinds, queries, keys, values, output_gradient)
+    )(tiles, kinds, queries, keys, values, output_gradient))
 
 
 def solution(mesh):

time: 158 us -> 142 us (0.90)
  Pallas kernels: 151 us -> 139 us
  local copies, waits for them, and re-layouts: 4.37 us -> 0 us
    pallas_call x1, Pallas kernels: 151 us -> 137 us  [body(): pl.pallas_call(kernel, name='attention_grads', out_shape=(jax.ShapeDtypeS...]
    unnamed x7 -> x0, local copies, waits for them, and re-layouts: 4.37 us -> none
    pallas_call x0 -> x1, Pallas kernels: none -> 2.46 us  [copy_out(): pl.pallas_call(copy_kernel, name='copy_out', out_shape=tuple((jax.ShapeDt...]
where the time goes in v4:
time: 142 us; the launch traced here: 140 us
  Pallas kernels  139 us (98%)
    pallas_call x1, Pallas kernels, body(): pl.pallas_call(kernel, name='attention_grads', out_shape=(jax.ShapeDtypeS...  137 us

profile of v4, /device:TPU:2, one launch (start us, length us, event | category | flops | bytes accessed | tf_op | source)
XLA Modules:
  0.0 139.9 jit_solution(3885933536439455904)
XLA Ops:
  0.6 136.8 %attention_grads.1 = (bf16[128,4096]{1,0:T(8,128)(2,1)}, bf16[128,2048]{1,0:T(8,128)(2,1)}, bf16[128,2048]{1,0:T(8,128)(2,1)}) custom-call(s32[8,6]{1,0:T(8,128)} %tiles_ref.1, s32[8,6]{1,0:T(8,128)} %kinds_ref.1, bf16[128,4096]{1,0:T(8,128)(2,1)} %q_in.1, bf16[128,2048]{1,0:T(8,128)(2,1)} %k_in.1, bf16[128,2048]{1,0:T(8,128)(2,1)} %v_in.1, ...), custom_call_target="tpu_custom_call" | custom-call | tf_op jit(solution)/shard_map/attention_grads/pallas_call | solution.py:428
  137.4 2.5 %copy_out.1 = (bf16[128,4096]{1,0:T(8,128)(2,1)}, bf16[128,2048]{1,0:T(8,128)(2,1)}, bf16[128,2048]{1,0:T(8,128)(2,1)}) custom-call(bf16[128,4096]{1,0:T(8,128)(2,1)} %get-tuple-element.6.refs_0_, bf16[128,2048]{1,0:T(8,128)(2,1)} %get-tuple-element.7.refs_1_, bf16[128,2048]{1,0:T(8,128)(2,1)} %get-tuple-element.8.refs_2_), custom_call_target="tpu_custom_call" | custom-call | tf_op jit(solution)/shard_map/copy_out/pallas_call | solution.py:409

commit v5 on v4

--- a/solution.py
+++ b/solution.py
@@ -329,7 +329,7 @@
             total[unit] = add(summed[unit, quad(0, z_hi)], mid[unit], back[unit])
         ref = ov_ref if unit % 2 else ok_ref
         there = ref.at[:, columns((x * HEADS + unit // 2) * HEAD, HEAD)]
-        for d in (1, 2, 3):
+        for d in (2, 1, 3):
             out_x.append(
                 send(total.at[unit, lax.rem(x + d, 4)], there, (ys, yr), unit * 3 + d - 1,
                      along_x[d - 1])

time: 142 us -> 142 us (level)
  no operation moved by 1% of the time
where the time goes in v5:
time: 142 us; the launch traced here: 140 us
  Pallas kernels  139 us (98%)
    pallas_call x1, Pallas kernels, body(): pl.pallas_call(kernel, name='attention_grads', out_shape=(jax.ShapeDtypeS...  137 us

profile of v5, /device:TPU:2, one launch (start us, length us, event | category | flops | bytes accessed | tf_op | source)
XLA Modules:
  0.0 139.8 jit_solution(13297975330607270765)
XLA Ops:
  0.6 136.7 %attention_grads.1 = (bf16[128,4096]{1,0:T(8,128)(2,1)}, bf16[128,2048]{1,0:T(8,128)(2,1)}, bf16[128,2048]{1,0:T(8,128)(2,1)}) custom-call(s32[8,6]{1,0:T(8,128)} %tiles_ref.1, s32[8,6]{1,0:T(8,128)} %kinds_ref.1, bf16[128,4096]{1,0:T(8,128)(2,1)} %q_in.1, bf16[128,2048]{1,0:T(8,128)(2,1)} %k_in.1, bf16[128,2048]{1,0:T(8,128)(2,1)} %v_in.1, ...), custom_call_target="tpu_custom_call" | custom-call | tf_op jit(solution)/shard_map/attention_grads/pallas_call | solution.py:428
  137.4 2.5 %copy_out.1 = (bf16[128,4096]{1,0:T(8,128)(2,1)}, bf16[128,2048]{1,0:T(8,128)(2,1)}, bf16[128,2048]{1,0:T(8,128)(2,1)}) custom-call(bf16[128,4096]{1,0:T(8,128)(2,1)} %get-tuple-element.6.refs_0_, bf16[128,2048]{1,0:T(8,128)(2,1)} %get-tuple-element.7.refs_1_, bf16[128,2048]{1,0:T(8,128)(2,1)} %get-tuple-element.8.refs_2_), custom_call_target="tpu_custom_call" | custom-call | tf_op jit(solution)/shard_map/copy_out/pallas_call | solution.py:409
